TPU v7x, 32 devices: a whole 2x2x4 slice. The times are simulated.
32 devices in a mesh: gx: 4 (over y, core), gy: 2 (over x), gz: 4 (over z).
Axes of the slice: x: 2, y: 2, z: 4, core: 2. Of those that a mesh axis runs over, the one named last changes fastest.
Arguments:
- features: bfloat16 [8, 2, 16, 128, 128], P('gx', 'gy', 'gz'), may hold values from -6 to 6
- msg_weight: bfloat16 [128, 128], replicated, may hold values from -0.5 to 0.5
- self_weight: bfloat16 [128, 128], replicated, may hold values from -0.5 to 0.5
- charge_weight: bfloat16 [128], replicated, may hold values from -0.5 to 0.5
- spline_corner: int32 [8, 2, 16, 3, 128], P('gx', 'gy', 'gz'), may hold values from 0 to 12
- spline_fraction: float32 [8, 2, 16, 3, 128], P('gx', 'gy', 'gz'), may hold values from 0 to 1
Outputs:
- feature_grad: float32 [8, 2, 16, 128, 128], P('gx', 'gy', 'gz')
- atom_potential: float32 [8, 2, 16, 128], P('gx', 'gy', 'gz')
- energy_per_atom: float32 [], replicated
All inputs are finite; a program needn't handle non-finite values.
Results may differ from a plain program's by a relative error of at most 0.0095.
Values may be sent and summed in bfloat16 or wider, within the bound.
A program may use at most 64 MiB of HBM per device.

v0:
```python
import math

import jax
import jax.numpy as jnp
from jax import lax
from jax.sharding import PartitionSpec as P

PC = 16


pair_scale = 0.1
coupling = 0.125
spread_width = 0.0625
highest = lax.Precision.HIGHEST


def with_halo(shard, sides, width):
    for axis, dim in sides:
        devices, length = (lax.axis_size(axis), shard.shape[dim])
        up = [(i, (i + 1) % devices) for i in range(devices)]
        down = [(j, i) for i, j in up]
        last = lax.slice_in_dim(shard, length - width, length, axis=dim)
        initial = lax.slice_in_dim(shard, 0, width, axis=dim)
        before = lax.ppermute(last, axis, up)
        after = lax.ppermute(initial, axis, down)
        shard = jnp.concatenate([before, shard, after], axis=dim)
    return shard


def spline_rows(corner, fraction, mesh_points):
    offset = jnp.arange(mesh_points, dtype=jnp.int32) - corner[..., None]
    within = fraction[..., None]
    first_weight = (1.0 - within) ** 3 / 6.0
    second_weight = (3.0 * within**3 - 6.0 * within**2 + 4.0) / 6.0
    third_weight = (-3.0 * within**3 + 3.0 * within**2 + 3.0 * within + 1.0) / 6.0
    fourth_weight = within**3 / 6.0
    nothing = jnp.zeros_like(first_weight)
    return jnp.where(
        offset == 0,
        first_weight,
        jnp.where(
            offset == 1,
            second_weight,
            jnp.where(offset == 2, third_weight, jnp.where(offset == 3, fourth_weight, nothing)),
        ),
    )


def pair_weights(centre, neighbour, offset):
    centre = centre.astype(jnp.float32)
    neighbour = neighbour.astype(jnp.float32)
    squared = None
    for which in range(3):
        gap = offset[which] + (neighbour[..., which, None, :] - centre[..., which, :, None])
        squared = gap * gap if squared is None else squared + gap * gap
    inside = jnp.maximum(1.0 - squared, 0.0)
    return (pair_scale * inside * inside).astype(jnp.bfloat16)


def all_offsets():
    return [
        (first, second, third)
        for first in (-1, 0, 1)
        for second in (-1, 0, 1)
        for third in (-1, 0, 1)
    ]


def near_block(padded, offset, cells):
    return padded[
        1 + offset[0] : 1 + offset[0] + cells[0],
        1 + offset[1] : 1 + offset[1] + cells[1],
        1 + offset[2] : 1 + offset[2] + cells[2],
    ]


def local_pairs(position, padded_position, padded_values):
    cells = position.shape[:3]
    total = jnp.zeros(cells + (position.shape[-1], padded_values.shape[-1]), jnp.float32)
    for offset in all_offsets():
        weights = pair_weights(position, near_block(padded_position, offset, cells), offset)
        total = total + jnp.einsum(
            "abcsn,abcnd->abcsd",
            weights,
            near_block(padded_values, offset, cells),
            preferred_element_type=jnp.float32,
        )
    return total


def spread_cells(charge, rows):
    points = rows[0].shape[-1]
    left = charge[..., None] * rows[0]
    right = (rows[1][..., :, None] * rows[2][..., None, :]).reshape(
        rows[1].shape[:-1] + (points * points,)
    )
    block = jnp.einsum("abcsi,abcsj->abcij", left, right, precision=highest)
    return block.reshape(block.shape[:-1] + (points, points))


def interpolate(cell_field, rows):
    points = rows[0].shape[-1]
    right = (rows[1][..., :, None] * rows[2][..., None, :]).reshape(
        rows[1].shape[:-1] + (points * points,)
    )
    flat_field = cell_field.reshape(cell_field.shape[:3] + (points, points * points))
    partial_value = jnp.einsum("abcij,abcsj->abcsi", flat_field, right, precision=highest)
    return jnp.sum(partial_value * rows[0], axis=-1)


def cells_to_mesh(block):
    count_a, count_b, count_c, points = (
        block.shape[0],
        block.shape[1],
        block.shape[2],
        block.shape[3],
    )
    return block.transpose(0, 3, 1, 4, 2, 5).reshape(
        count_a * points, count_b * points, count_c * points
    )


def mesh_to_cells(field, count_a, count_b, count_c):
    points = field.shape[0] // count_a
    return field.reshape(count_a, points, count_b, points, count_c, points).transpose(
        0, 2, 4, 1, 3, 5
    )


def influence_of(index_x, index_y, index_z, size_x, size_y, size_z, points):

    def wave(index, size):
        signed = jnp.where(2 * index >= size, index - size, index)
        return signed.astype(jnp.float32) * (points / size)

    wave_x = wave(index_x, size_x)
    wave_y = wave(index_y, size_y)
    wave_z = wave(index_z, size_z)
    squared = wave_x * wave_x + wave_y * wave_y + wave_z * wave_z
    safe = jnp.where(squared > 0, squared, 1.0)
    return jnp.where(squared > 0, jnp.exp(-((math.pi * spread_width) ** 2) * squared) / safe, 0.0)


def twiddle(first_index, second_index, length):
    turns = first_index[:, None] * second_index[None, :] % length
    angle = 2.0 * math.pi / length * turns.astype(jnp.float32)
    return (jnp.cos(angle), jnp.sin(angle))


def reciprocal(mesh, natoms):
    local_x, local_y, local_z = mesh.shape
    count_x = lax.axis_size("gx")
    count_y = lax.axis_size("gy")
    count_z = lax.axis_size("gz")
    size_x = local_x * count_x
    size_y = local_y * count_y
    size_z = local_z * count_z
    natural_x = jnp.arange(size_x, dtype=jnp.int32)
    natural_y = jnp.arange(size_y, dtype=jnp.int32)
    natural_z = jnp.arange(size_z, dtype=jnp.int32)
    depth = lax.all_to_all(mesh, "gz", split_axis=0, concat_axis=2, tiled=True)
    cos_z, sin_z = twiddle(natural_z, natural_z, size_z)
    real_part = jnp.einsum("xyz,zk->xyk", depth, cos_z, precision=highest)
    imag_part = -jnp.einsum("xyz,zk->xyk", depth, sin_z, precision=highest)
    real_part, imag_part = (
        lax.all_to_all(real_part, "gy", split_axis=2, concat_axis=1, tiled=True),
        lax.all_to_all(imag_part, "gy", split_axis=2, concat_axis=1, tiled=True),
    )
    cos_y, sin_y = twiddle(natural_y, natural_y, size_y)
    real_part, imag_part = (
        jnp.einsum("xyz,yk->xkz", real_part, cos_y, precision=highest)
        + jnp.einsum("xyz,yk->xkz", imag_part, sin_y, precision=highest),
        jnp.einsum("xyz,yk->xkz", imag_part, cos_y, precision=highest)
        - jnp.einsum("xyz,yk->xkz", real_part, sin_y, precision=highest),
    )
    real_part, imag_part = (
        lax.all_to_all(real_part, ("gx", "gz"), split_axis=1, concat_axis=0, tiled=True),
        lax.all_to_all(imag_part, ("gx", "gz"), split_axis=1, concat_axis=0, tiled=True),
    )
    cos_in, sin_in = twiddle(natural_x, natural_x, size_x)
    real_part, imag_part = (
        jnp.einsum("xyz,xk->kyz", real_part, cos_in, precision=highest)
        + jnp.einsum("xyz,xk->kyz", imag_part, sin_in, precision=highest),
        jnp.einsum("xyz,xk->kyz", imag_part, cos_in, precision=highest)
        - jnp.einsum("xyz,xk->kyz", real_part, sin_in, precision=highest),
    )
    band_y = real_part.shape[1]
    band_z = real_part.shape[2]
    index_y = lax.axis_index(("gx", "gz")) * band_y + jnp.arange(band_y, dtype=jnp.int32)
    index_z = lax.axis_index("gy") * band_z + jnp.arange(band_z, dtype=jnp.int32)
    influence = influence_of(
        natural_x[:, None, None],
        index_y[None, :, None],
        index_z[None, None, :],
        size_x,
        size_y,
        size_z,
        PC,
    )
    volume = size_x // PC * (size_y // PC) * (size_z // PC)
    energy_part = jnp.sum(influence * (real_part * real_part + imag_part * imag_part))
    total = lax.psum(energy_part, ("gx", "gy", "gz"))
    energy = coupling / (2.0 * volume * natoms) * total
    scaled_real = influence * real_part
    scaled_imag = influence * imag_part
    cos_x, sin_x = twiddle(natural_x, natural_x, size_x)
    out_real = jnp.einsum("kyz,kx->xyz", scaled_real, cos_x, precision=highest) - jnp.einsum(
        "kyz,kx->xyz", scaled_imag, sin_x, precision=highest
    )
    out_imag = jnp.einsum("kyz,kx->xyz", scaled_real, sin_x, precision=highest) + jnp.einsum(
        "kyz,kx->xyz", scaled_imag, cos_x, precision=highest
    )
    out_real, out_imag = (
        lax.all_to_all(out_real, ("gx", "gz"), split_axis=0, concat_axis=1, tiled=True),
        lax.all_to_all(out_imag, ("gx", "gz"), split_axis=0, concat_axis=1, tiled=True),
    )
    out_real, out_imag = (
        jnp.einsum("xkz,ky->xyz", out_real, cos_y, precision=highest)
        - jnp.einsum("xkz,ky->xyz", out_imag, sin_y, precision=highest),
        jnp.einsum("xkz,ky->xyz", out_real, sin_y, precision=highest)
        + jnp.einsum("xkz,ky->xyz", out_imag, cos_y, precision=highest),
    )
    out_real, out_imag = (
        lax.all_to_all(out_real, "gy", split_axis=1, concat_axis=2, tiled=True),
        lax.all_to_all(out_imag, "gy", split_axis=1, concat_axis=2, tiled=True),
    )
    field = jnp.einsum("xyk,kz->xyz", out_real, cos_z, precision=highest) - jnp.einsum(
        "xyk,kz->xyz", out_imag, sin_z, precision=highest
    )
    field = lax.all_to_all(field, "gz", split_axis=2, concat_axis=0, tiled=True)
    return (coupling / volume * field, energy)


def body(features, msg_weight, self_weight, charge_weight, spline_corner, spline_fraction):
    cells_x, cells_y, cells_z, slots, width = features.shape
    position = ((spline_corner.astype(jnp.float32) + 1.0 + spline_fraction) / PC).astype(
        jnp.bfloat16
    )
    flat = features.reshape(-1, width)
    projected = (
        jnp.dot(flat, msg_weight, preferred_element_type=jnp.float32)
        .astype(jnp.bfloat16)
        .reshape(features.shape)
    )
    padded_values, padded_position = (
        with_halo(projected, (("gx", 0), ("gy", 1), ("gz", 2)), 1),
        with_halo(position, (("gx", 0), ("gy", 1), ("gz", 2)), 1),
    )
    message = local_pairs(position, padded_position, padded_values)
    preact = (
        jnp.dot(flat, self_weight, preferred_element_type=jnp.float32).reshape(features.shape)
        + message
    )
    charge = jnp.sum(jax.nn.silu(preact) * charge_weight.astype(jnp.float32), axis=-1)
    rows = [
        spline_rows(spline_corner[..., which, :], spline_fraction[..., which, :], PC)
        for which in range(3)
    ]
    mesh = cells_to_mesh(spread_cells(charge, rows))
    natoms = (
        cells_x
        * cells_y
        * cells_z
        * slots
        * lax.axis_size("gx")
        * lax.axis_size("gy")
        * lax.axis_size("gz")
    )
    mesh_potential, energy = reciprocal(mesh, natoms)
    atom_potential = interpolate(mesh_to_cells(mesh_potential, cells_x, cells_y, cells_z), rows)
    sigma = jax.nn.sigmoid(preact)
    slope = sigma * (1.0 + preact * (1.0 - sigma))
    cotangent = (atom_potential[..., None] * charge_weight.astype(jnp.float32) * slope).astype(
        jnp.bfloat16
    )
    padded_cotangent = with_halo(cotangent, (("gx", 0), ("gy", 1), ("gz", 2)), 1)
    back_sum = local_pairs(position, padded_position, padded_cotangent)
    back_message = back_sum.astype(jnp.bfloat16)
    grad = jnp.dot(
        back_message.reshape(-1, width), msg_weight.T, preferred_element_type=jnp.float32
    )
    grad = grad + jnp.dot(
        cotangent.reshape(-1, width), self_weight.T, preferred_element_type=jnp.float32
    )
    return (grad.reshape(features.shape), atom_potential, energy)


def solution(mesh):
    in_specs = (
        P("gx", "gy", "gz", None, None),
        P(),
        P(),
        P(),
        P("gx", "gy", "gz", None, None),
        P("gx", "gy", "gz", None, None),
    )
    out_specs = (P("gx", "gy", "gz", None, None), P("gx", "gy", "gz", None), P())
    return jax.shard_map(body, mesh=mesh, in_specs=in_specs, out_specs=out_specs, check_vma=False)
```

profile of v0, /device:TPU:0, one launch (start us, length us, event | category | flops | bytes accessed | tf_op | source)
XLA Modules:
  0.0 309.3 jit_solution(1914827654386493689)
XLA Ops:
  26.2 11.2 %collective-permute-done.7 = bf16[4,1,4,128,128]{4,3,2,0,1:T(8,128)(2,1)S(1)} collective-permute-done((bf16[4,1,4,128,128]{4,3,2,0,1:T(8,128)(2,1)S(1)}, bf16[4,1,4,128,128]{4,3,2,0,1:T(8,128)(2,1)S(1)}, u32[]{:S(2)}, u32[]{:S(2)}) %collective-permute-start.7) | collective-permute-done | bytes 524320 | tf_op jit(solution)/shard_map/ppermute | solution.py:24
  37.3 7.8 %collective-permute-done.8 = bf16[4,1,4,128,128]{4,3,2,0,1:T(8,128)(2,1)S(1)} collective-permute-done((bf16[4,1,4,128,128]{4,3,2,0,1:T(8,128)(2,1)S(1)}, bf16[4,1,4,128,128]{4,3,2,0,1:T(8,128)(2,1)S(1)}, u32[]{:S(2)}, u32[]{:S(2)}) %collective-permute-start.8) | collective-permute-done | bytes 524320 | tf_op jit(solution)/shard_map/ppermute | solution.py:25
  45.2 3.6 %collective-permute-start.11 = (bf16[4,3,1,128,128]{4,3,2,0,1:T(8,128)(2,1)S(1)}, bf16[4,3,1,128,128]{4,3,2,0,1:T(8,128)(2,1)S(1)}, u32[]{:S(2)}, u32[]{:S(2)}) collective-permute-start(bf16[4,3,1,128,128]{4,3,2,0,1:T(8,128)(2,1)S(1)} %get-tuple-element.21), channel_id=1, source_target_pairs={{1,0},{2,1},{3,2},{0,3},{5,4},{6,5},{7,6},{4,7},{9,8},{10,9},{11,1... | collective-permute-start | bytes 1179656 | tf_op jit(solution)/shard_map/ppermute | solution.py:25
  53.8 4.3 %collective-permute-done.11 = bf16[4,3,1,128,128]{4,3,2,0,1:T(8,128)(2,1)S(1)} collective-permute-done((bf16[4,3,1,128,128]{4,3,2,0,1:T(8,128)(2,1)S(1)}, bf16[4,3,1,128,128]{4,3,2,0,1:T(8,128)(2,1)S(1)}, u32[]{:S(2)}, u32[]{:S(2)}) %collective-permute-start.11) | collective-permute-done | bytes 393248 | tf_op jit(solution)/shard_map/ppermute | solution.py:25
  58.1 4.9 %collective-permute-done.9 = bf16[4,3,1,128,128]{4,3,2,0,1:T(8,128)(2,1)S(1)} collective-permute-done((bf16[4,3,1,128,128]{4,3,2,0,1:T(8,128)(2,1)S(1)}, bf16[4,3,1,128,128]{4,3,2,0,1:T(8,128)(2,1)S(1)}, u32[]{:S(2)}, u32[]{:S(2)}) %collective-permute-start.9) | collective-permute-done | bytes 393248 | tf_op jit(solution)/shard_map/ppermute | solution.py:24
  84.5 3.5 %all-to-all-start = ((f32[4,1,8192]{2,1,0:T(1,128)}), f32[4,1,8192]{2,1,0:T(1,128)S(1)}, u32[]{:S(2)}, u32[]{:S(2)}) async-start(f32[4,1,8192]{2,1,0:T(1,128)} %reshape.1458), calls=%async_computation | async-start | bytes 262144 | tf_op jit(solution)/shard_map/all_to_all | solution.py:161
  88.0 5.8 %all-to-all-done = f32[4,1,8192]{2,1,0:T(1,128)S(1)} async-done(((f32[4,1,8192]{2,1,0:T(1,128)}), f32[4,1,8192]{2,1,0:T(1,128)S(1)}, u32[]{:S(2)}, u32[]{:S(2)}) %all-to-all-start) | async-done | bytes 131104 | tf_op jit(solution)/shard_map/all_to_all | solution.py:161
  98.7 3.4 %all-to-all-start.2 = ((f32[2,1,16384]{2,1,0:T(1,128)}), f32[2,1,16384]{2,1,0:T(1,128)S(1)}, u32[]{:S(2)}, u32[]{:S(2)}) async-start(f32[2,1,16384]{2,1,0:T(1,128)} %reshape.1462), calls=%async_computation.2 | async-start | bytes 262144 | tf_op jit(solution)/shard_map/all_to_all | solution.py:167
  106.5 3.4 %all-to-all-start.1 = ((f32[2,1,16384]{2,1,0:T(1,128)}), f32[2,1,16384]{2,1,0:T(1,128)S(1)}, u32[]{:S(2)}, u32[]{:S(2)}) async-start(f32[2,1,16384]{2,1,0:T(1,128)} %reshape.1460), calls=%async_computation.1 | async-start | bytes 262144 | tf_op jit(solution)/shard_map/all_to_all | solution.py:166
  117.6 3.5 %all-to-all-start.3 = ((f32[8,32,128]{2,0,1:T(8,128)}), f32[8,32,128]{2,0,1:T(8,128)S(1)}, u32[]{:S(2)}, u32[]{:S(2)}) async-start(f32[8,32,128]{2,0,1:T(8,128)} %copy.58), calls=%async_computation.3 | async-start | bytes 262144 | tf_op jit(solution)/shard_map/all_to_all | solution.py:177
  122.5 5.9 %all-to-all-done.3 = f32[8,32,128]{2,0,1:T(8,128)S(1)} async-done(((f32[8,32,128]{2,0,1:T(8,128)}), f32[8,32,128]{2,0,1:T(8,128)S(1)}, u32[]{:S(2)}, u32[]{:S(2)}) %all-to-all-start.3) | async-done | bytes 131104 | tf_op jit(solution)/shard_map/all_to_all | solution.py:177
  128.4 3.5 %all-to-all-start.4 = ((f32[8,32,128]{2,0,1:T(8,128)}), f32[8,32,128]{2,0,1:T(8,128)S(1)}, u32[]{:S(2)}, u32[]{:S(2)}) async-start(f32[8,32,128]{2,0,1:T(8,128)} %copy.60), calls=%async_computation.4 | async-start | bytes 262144 | tf_op jit(solution)/shard_map/all_to_all | solution.py:178
  132.5 6.8 %all-to-all-done.4 = f32[8,32,128]{2,0,1:T(8,128)S(1)} async-done(((f32[8,32,128]{2,0,1:T(8,128)}), f32[8,32,128]{2,0,1:T(8,128)S(1)}, u32[]{:S(2)}, u32[]{:S(2)}) %all-to-all-start.4) | async-done | bytes 131104 | tf_op jit(solution)/shard_map/all_to_all | solution.py:178
  143.4 3.9 %all-to-all-start.5 = ((f32[128,2,128]{2,1,0:T(2,128)}), f32[128,2,128]{2,1,0:T(2,128)S(1)}, u32[]{:S(2)}, u32[]{:S(2)}) async-start(f32[128,2,128]{2,1,0:T(2,128)} %copy.62), calls=%async_computation.5 | async-start | bytes 262144 | tf_op jit(solution)/shard_map/all_to_all | solution.py:214
  149.3 5.4 %all-to-all-done.5 = f32[128,2,128]{2,1,0:T(2,128)S(1)} async-done(((f32[128,2,128]{2,1,0:T(2,128)}), f32[128,2,128]{2,1,0:T(2,128)S(1)}, u32[]{:S(2)}, u32[]{:S(2)}) %all-to-all-start.5) | async-done | bytes 131104 | tf_op jit(solution)/shard_map/all_to_all | solution.py:214
  154.7 3.5 %all-to-all-start.6 = ((f32[128,2,128]{2,1,0:T(2,128)}), f32[128,2,128]{2,1,0:T(2,128)S(1)}, u32[]{:S(2)}, u32[]{:S(2)}) async-start(f32[128,2,128]{2,1,0:T(2,128)} %copy.64), calls=%async_computation.6 | async-start | bytes 262144 | tf_op jit(solution)/shard_map/all_to_all | solution.py:215
  158.9 6.6 %all-to-all-done.6 = f32[128,2,128]{2,1,0:T(2,128)S(1)} async-done(((f32[128,2,128]{2,1,0:T(2,128)}), f32[128,2,128]{2,1,0:T(2,128)S(1)}, u32[]{:S(2)}, u32[]{:S(2)}) %all-to-all-start.6) | async-done | bytes 131104 | tf_op jit(solution)/shard_map/all_to_all | solution.py:215
  174.5 3.4 %all-to-all-start.7 = ((f32[8,32,128]{2,0,1:T(8,128)}), f32[8,32,128]{2,0,1:T(8,128)S(1)}, u32[]{:S(2)}, u32[]{:S(2)}) async-start(f32[8,32,128]{2,0,1:T(8,128)} %copy.66), calls=%async_computation.7 | async-start | bytes 262144 | tf_op jit(solution)/shard_map/all_to_all | solution.py:224
  178.1 4.2 %all-to-all-done.7 = f32[8,32,128]{2,0,1:T(8,128)S(1)} async-done(((f32[8,32,128]{2,0,1:T(8,128)}), f32[8,32,128]{2,0,1:T(8,128)S(1)}, u32[]{:S(2)}, u32[]{:S(2)}) %all-to-all-start.7) | async-done | bytes 131104 | tf_op jit(solution)/shard_map/all_to_all | solution.py:224
  189.9 39.9 %psum.7 = f32[]{:T(128)} all-reduce(f32[]{:T(128)} %get-tuple-element.154), channel_id=1, replica_groups=mesh['gx'=4,'gy'=2,'gz'=4] {'gx','gy','gz'}, use_global_device_ids=true, to_apply=%region_3.4 | all-reduce | flops 1 | bytes 8 | tf_op jit(solution)/shard_map/psum | solution.py:202
  248.8 9.8 %collective-permute-done.14 = bf16[4,1,4,128,128]{4,3,2,0,1:T(8,128)(2,1)S(1)} collective-permute-done((bf16[4,1,4,128,128]{4,3,2,0,1:T(8,128)(2,1)S(1)}, bf16[4,1,4,128,128]{4,3,2,0,1:T(8,128)(2,1)S(1)}, u32[]{:S(2)}, u32[]{:S(2)}) %collective-permute-start.14) | collective-permute-done | bytes 524320 | tf_op jit(solution)/shard_map/ppermute | solution.py:24
  258.7 11.2 %collective-permute-done.15 = bf16[4,1,4,128,128]{4,3,2,0,1:T(8,128)(2,1)S(1)} collective-permute-done((bf16[4,1,4,128,128]{4,3,2,0,1:T(8,128)(2,1)S(1)}, bf16[4,1,4,128,128]{4,3,2,0,1:T(8,128)(2,1)S(1)}, u32[]{:S(2)}, u32[]{:S(2)}) %collective-permute-start.15) | collective-permute-done | bytes 524320 | tf_op jit(solution)/shard_map/ppermute | solution.py:25
  278.8 5.1 %collective-permute-done.16 = bf16[4,3,1,128,128]{4,3,2,0,1:T(8,128)(2,1)S(1)} collective-permute-done((bf16[4,3,1,128,128]{4,3,2,0,1:T(8,128)(2,1)S(1)}, bf16[4,3,1,128,128]{4,3,2,0,1:T(8,128)(2,1)S(1)}, u32[]{:S(2)}, u32[]{:S(2)}) %collective-permute-start.16) | collective-permute-done | bytes 393248 | tf_op jit(solution)/shard_map/ppermute | solution.py:24
  283.9 7.3 %collective-permute-done.17 = bf16[4,3,1,128,128]{4,3,2,0,1:T(8,128)(2,1)S(1)} collective-permute-done((bf16[4,3,1,128,128]{4,3,2,0,1:T(8,128)(2,1)S(1)}, bf16[4,3,1,128,128]{4,3,2,0,1:T(8,128)(2,1)S(1)}, u32[]{:S(2)}, u32[]{:S(2)}) %collective-permute-start.17) | collective-permute-done | bytes 393248 | tf_op jit(solution)/shard_map/ppermute | solution.py:25
  (217 shorter events, 137.7 us)
Async XLA Ops:
  1.4 8.8 %collective-permute-start = (bf16[1,1,4,3,128]{4,2,3,1,0:T(4,128)(2,1)S(1)}, bf16[1,1,4,3,128]{4,2,3,1,0:T(4,128)(2,1)S(1)}, u32[]{:S(2)}, u32[]{:S(2)}) collective-permute-start(bf16[1,1,4,3,128]{4,2,3,1,0:T(4,128)(2,1)S(1)} %get-tuple-element.150), channel_id=1, source_target_pairs={{0,8},{8,16},{16,24},{24,0},{1,9},{9,17},{17,25},{25,1},{2,10},{10... | collective-permute-start | bytes 9224 | tf_op jit(solution)/shard_map/ppermute | solution.py:24
  2.0 8.3 %collective-permute-start.1 = (bf16[1,1,4,3,128]{4,2,3,1,0:T(4,128)(2,1)S(1)}, bf16[1,1,4,3,128]{4,2,3,1,0:T(4,128)(2,1)S(1)}, u32[]{:S(2)}, u32[]{:S(2)}) collective-permute-start(bf16[1,1,4,3,128]{4,2,3,1,0:T(4,128)(2,1)S(1)} %get-tuple-element.151), channel_id=1, source_target_pairs={{8,0},{16,8},{24,16},{0,24},{9,1},{17,9},{25,17},{1,25},{10,2},{18... | collective-permute-start | bytes 9224 | tf_op jit(solution)/shard_map/ppermute | solution.py:25
  5.0 17.4 %collective-permute-start.5 = (bf16[1,1,4,128,128]{4,3,2,0,1:T(8,128)(2,1)S(1)}, bf16[1,1,4,128,128]{4,3,2,0,1:T(8,128)(2,1)S(1)}, u32[]{:S(2)}, u32[]{:S(2)}) collective-permute-start(bf16[1,1,4,128,128]{4,3,2,0,1:T(8,128)(2,1)S(1)} %bitcast.602), channel_id=1, source_target_pairs={{0,8},{8,16},{16,24},{24,0},{1,9},{9,17},{17,25},{25,1},{2,10},{10... | collective-permute-start | bytes 393224 | tf_op jit(solution)/shard_map/ppermute | solution.py:24
  5.7 16.7 %collective-permute-start.6 = (bf16[1,1,4,128,128]{4,3,2,0,1:T(8,128)(2,1)S(1)}, bf16[1,1,4,128,128]{4,3,2,0,1:T(8,128)(2,1)S(1)}, u32[]{:S(2)}, u32[]{:S(2)}) collective-permute-start(bf16[1,1,4,128,128]{4,3,2,0,1:T(8,128)(2,1)S(1)} %bitcast.601), channel_id=1, source_target_pairs={{8,0},{16,8},{24,16},{0,24},{9,1},{17,9},{25,17},{1,25},{10,2},{18... | collective-permute-start | bytes 393224 | tf_op jit(solution)/shard_map/ppermute | solution.py:25
  16.3 5.6 %collective-permute-start.4 = (bf16[4,3,1,3,128]{4,2,3,1,0:T(2,128)(2,1)S(1)}, bf16[4,3,1,3,128]{4,2,3,1,0:T(2,128)(2,1)S(1)}, u32[]{:S(2)}, u32[]{:S(2)}) collective-permute-start(bf16[4,3,1,3,128]{4,2,3,1,0:T(2,128)(2,1)S(1)} %get-tuple-element.44), channel_id=1, source_target_pairs={{0,1},{1,2},{2,3},{3,0},{4,5},{5,6},{6,7},{7,4},{8,9},{9,10},{10,1... | collective-permute-start | bytes 27656 | tf_op jit(solution)/shard_map/ppermute | solution.py:24
  22.5 14.9 %collective-permute-start.7 = (bf16[4,1,4,128,128]{4,3,2,0,1:T(8,128)(2,1)S(1)}, bf16[4,1,4,128,128]{4,3,2,0,1:T(8,128)(2,1)S(1)}, u32[]{:S(2)}, u32[]{:S(2)}) collective-permute-start(bf16[4,1,4,128,128]{4,3,2,0,1:T(8,128)(2,1)S(1)} %pad_maximum_fusion.2), channel_id=1, source_target_pairs={{0,4},{4,0},{1,5},{5,1},{2,6},{6,2},{3,7},{7,3},{8,12},{12,8},{9,1... | collective-permute-start | bytes 1572872 | tf_op jit(solution)/shard_map/ppermute | solution.py:24
  23.0 22.1 %collective-permute-start.8 = (bf16[4,1,4,128,128]{4,3,2,0,1:T(8,128)(2,1)S(1)}, bf16[4,1,4,128,128]{4,3,2,0,1:T(8,128)(2,1)S(1)}, u32[]{:S(2)}, u32[]{:S(2)}) collective-permute-start(bf16[4,1,4,128,128]{4,3,2,0,1:T(8,128)(2,1)S(1)} %pad_maximum_fusion.2), channel_id=1, source_target_pairs={{4,0},{0,4},{5,1},{1,5},{6,2},{2,6},{7,3},{3,7},{12,8},{8,12},{13,... | collective-permute-start | bytes 1572872 | tf_op jit(solution)/shard_map/ppermute | solution.py:25
  45.2 12.9 %collective-permute-start.11 = (bf16[4,3,1,128,128]{4,3,2,0,1:T(8,128)(2,1)S(1)}, bf16[4,3,1,128,128]{4,3,2,0,1:T(8,128)(2,1)S(1)}, u32[]{:S(2)}, u32[]{:S(2)}) collective-permute-start(bf16[4,3,1,128,128]{4,3,2,0,1:T(8,128)(2,1)S(1)} %get-tuple-element.21), channel_id=1, source_target_pairs={{1,0},{2,1},{3,2},{0,3},{5,4},{6,5},{7,6},{4,7},{9,8},{10,9},{11,1... | collective-permute-start | bytes 1179656 | tf_op jit(solution)/shard_map/ppermute | solution.py:25
  48.8 14.2 %collective-permute-start.9 = (bf16[4,3,1,128,128]{4,3,2,0,1:T(8,128)(2,1)S(1)}, bf16[4,3,1,128,128]{4,3,2,0,1:T(8,128)(2,1)S(1)}, u32[]{:S(2)}, u32[]{:S(2)}) collective-permute-start(bf16[4,3,1,128,128]{4,3,2,0,1:T(8,128)(2,1)S(1)} %get-tuple-element.20), channel_id=1, source_target_pairs={{0,1},{1,2},{2,3},{3,0},{4,5},{5,6},{6,7},{7,4},{8,9},{9,10},{10,1... | collective-permute-start | bytes 1179656 | tf_op jit(solution)/shard_map/ppermute | solution.py:24
  84.5 9.4 %all-to-all-start = ((f32[4,1,8192]{2,1,0:T(1,128)}), f32[4,1,8192]{2,1,0:T(1,128)S(1)}, u32[]{:S(2)}, u32[]{:S(2)}) async-start(f32[4,1,8192]{2,1,0:T(1,128)} %reshape.1458), calls=%async_computation | async-start | bytes 262144 | tf_op jit(solution)/shard_map/all_to_all | solution.py:161
  98.7 7.8 %all-to-all-start.2 = ((f32[2,1,16384]{2,1,0:T(1,128)}), f32[2,1,16384]{2,1,0:T(1,128)S(1)}, u32[]{:S(2)}, u32[]{:S(2)}) async-start(f32[2,1,16384]{2,1,0:T(1,128)} %reshape.1462), calls=%async_computation.2 | async-start | bytes 262144 | tf_op jit(solution)/shard_map/all_to_all | solution.py:167
  106.5 7.8 %all-to-all-start.1 = ((f32[2,1,16384]{2,1,0:T(1,128)}), f32[2,1,16384]{2,1,0:T(1,128)S(1)}, u32[]{:S(2)}, u32[]{:S(2)}) async-start(f32[2,1,16384]{2,1,0:T(1,128)} %reshape.1460), calls=%async_computation.1 | async-start | bytes 262144 | tf_op jit(solution)/shard_map/all_to_all | solution.py:166
  117.6 10.9 %all-to-all-start.3 = ((f32[8,32,128]{2,0,1:T(8,128)}), f32[8,32,128]{2,0,1:T(8,128)S(1)}, u32[]{:S(2)}, u32[]{:S(2)}) async-start(f32[8,32,128]{2,0,1:T(8,128)} %copy.58), calls=%async_computation.3 | async-start | bytes 262144 | tf_op jit(solution)/shard_map/all_to_all | solution.py:177
  128.4 10.9 %all-to-all-start.4 = ((f32[8,32,128]{2,0,1:T(8,128)}), f32[8,32,128]{2,0,1:T(8,128)S(1)}, u32[]{:S(2)}, u32[]{:S(2)}) async-start(f32[8,32,128]{2,0,1:T(8,128)} %copy.60), calls=%async_computation.4 | async-start | bytes 262144 | tf_op jit(solution)/shard_map/all_to_all | solution.py:178
  143.4 11.3 %all-to-all-start.5 = ((f32[128,2,128]{2,1,0:T(2,128)}), f32[128,2,128]{2,1,0:T(2,128)S(1)}, u32[]{:S(2)}, u32[]{:S(2)}) async-start(f32[128,2,128]{2,1,0:T(2,128)} %copy.62), calls=%async_computation.5 | async-start | bytes 262144 | tf_op jit(solution)/shard_map/all_to_all | solution.py:214
  154.7 10.9 %all-to-all-start.6 = ((f32[128,2,128]{2,1,0:T(2,128)}), f32[128,2,128]{2,1,0:T(2,128)S(1)}, u32[]{:S(2)}, u32[]{:S(2)}) async-start(f32[128,2,128]{2,1,0:T(2,128)} %copy.64), calls=%async_computation.6 | async-start | bytes 262144 | tf_op jit(solution)/shard_map/all_to_all | solution.py:215
  166.7 7.8 %all-to-all-start.8 = ((f32[8,32,128]{2,0,1:T(8,128)}), f32[8,32,128]{2,0,1:T(8,128)S(1)}, u32[]{:S(2)}, u32[]{:S(2)}) async-start(f32[8,32,128]{2,0,1:T(8,128)} %copy.68), calls=%async_computation.8 | async-start | bytes 262144 | tf_op jit(solution)/shard_map/all_to_all | solution.py:225
  174.5 7.8 %all-to-all-start.7 = ((f32[8,32,128]{2,0,1:T(8,128)}), f32[8,32,128]{2,0,1:T(8,128)S(1)}, u32[]{:S(2)}, u32[]{:S(2)}) async-start(f32[8,32,128]{2,0,1:T(8,128)} %copy.66), calls=%async_computation.7 | async-start | bytes 262144 | tf_op jit(solution)/shard_map/all_to_all | solution.py:224
  186.6 43.9 %all-to-all-start.9 = ((f32[4,1,8192]{2,1,0:T(1,128)}), f32[4,1,8192]{2,1,0:T(1,128)S(1)}, u32[]{:S(2)}, u32[]{:S(2)}) async-start(f32[4,1,8192]{2,1,0:T(1,128)} %reshape.1464), calls=%async_computation.9 | async-start | bytes 262144 | tf_op jit(solution)/shard_map/all_to_all | solution.py:230
  238.8 5.5 %collective-permute-start.13 = (bf16[1,1,4,128,128]{4,3,2,1,0:T(8,128)(2,1)S(1)}, bf16[1,1,4,128,128]{4,3,2,1,0:T(8,128)(2,1)S(1)}, u32[]{:S(2)}, u32[]{:S(2)}) collective-permute-start(bf16[1,1,4,128,128]{4,3,2,1,0:T(8,128)(2,1)S(1)} %get-tuple-element.23), channel_id=1, source_target_pairs={{8,0},{16,8},{24,16},{0,24},{9,1},{17,9},{25,17},{1,25},{10,2},{18... | collective-permute-start | bytes 393224 | tf_op jit(solution)/shard_map/ppermute | solution.py:25
  244.3 14.3 %collective-permute-start.14 = (bf16[4,1,4,128,128]{4,3,2,0,1:T(8,128)(2,1)S(1)}, bf16[4,1,4,128,128]{4,3,2,0,1:T(8,128)(2,1)S(1)}, u32[]{:S(2)}, u32[]{:S(2)}) collective-permute-start(bf16[4,1,4,128,128]{4,3,2,0,1:T(8,128)(2,1)S(1)} %pad_maximum_fusion.3), channel_id=1, source_target_pairs={{0,4},{4,0},{1,5},{5,1},{2,6},{6,2},{3,7},{7,3},{8,12},{12,8},{9,1... | collective-permute-start | bytes 1572872 | tf_op jit(solution)/shard_map/ppermute | solution.py:24
  245.6 24.3 %collective-permute-start.15 = (bf16[4,1,4,128,128]{4,3,2,0,1:T(8,128)(2,1)S(1)}, bf16[4,1,4,128,128]{4,3,2,0,1:T(8,128)(2,1)S(1)}, u32[]{:S(2)}, u32[]{:S(2)}) collective-permute-start(bf16[4,1,4,128,128]{4,3,2,0,1:T(8,128)(2,1)S(1)} %pad_maximum_fusion.3), channel_id=1, source_target_pairs={{4,0},{0,4},{5,1},{1,5},{6,2},{2,6},{7,3},{3,7},{12,8},{8,12},{13,... | collective-permute-start | bytes 1572872 | tf_op jit(solution)/shard_map/ppermute | solution.py:25
  270.0 13.9 %collective-permute-start.16 = (bf16[4,3,1,128,128]{4,3,2,0,1:T(8,128)(2,1)S(1)}, bf16[4,3,1,128,128]{4,3,2,0,1:T(8,128)(2,1)S(1)}, u32[]{:S(2)}, u32[]{:S(2)}) collective-permute-start(bf16[4,3,1,128,128]{4,3,2,0,1:T(8,128)(2,1)S(1)} %get-tuple-element.16), channel_id=1, source_target_pairs={{0,1},{1,2},{2,3},{3,0},{4,5},{5,6},{6,7},{7,4},{8,9},{9,10},{10,1... | collective-permute-start | bytes 1179656 | tf_op jit(solution)/shard_map/ppermute | solution.py:24
  271.5 19.7 %collective-permute-start.17 = (bf16[4,3,1,128,128]{4,3,2,0,1:T(8,128)(2,1)S(1)}, bf16[4,3,1,128,128]{4,3,2,0,1:T(8,128)(2,1)S(1)}, u32[]{:S(2)}, u32[]{:S(2)}) collective-permute-start(bf16[4,3,1,128,128]{4,3,2,0,1:T(8,128)(2,1)S(1)} %get-tuple-element.17), channel_id=1, source_target_pairs={{1,0},{2,1},{3,2},{0,3},{5,4},{6,5},{7,6},{4,7},{9,8},{10,9},{11,1... | collective-permute-start | bytes 1179656 | tf_op jit(solution)/shard_map/ppermute | solution.py:25
  (10 other events, 34.8 us)
where the time goes:
time: 314 us; the launch traced here: 309 us
  waiting for transfers between devices  113 us (36%)
  matrix products  62.1 us (20%)
  starting transfers between devices  59.2 us (19%)
  blocking collectives  39.9 us (13%)
  local copies, waits for them, and re-layouts  22.5 us (7%)
  other arithmetic  9.17 us (3%)
  between operations  3.53 us (1%)
    dot_general x54, matrix products, local_pairs(): jnp.einsum('abcsn,abcnd->abcsd', weights, near_block(padded_values, offse...  44.5 us
    psum x1, blocking collectives, reciprocal(): total = lax.psum(energy_part, ('gx', 'gy', 'gz'))  39.9 us
    ppermute x9, waiting for transfers between devices, with_halo(): before = lax.ppermute(last, axis, up)  36.7 us
    ppermute x9, waiting for transfers between devices, with_halo(): after = lax.ppermute(initial, axis, down)  33.8 us
    ppermute x9, starting transfers between devices, with_halo(): after = lax.ppermute(initial, axis, down)  15.7 us
    ppermute x9, starting transfers between devices, with_halo(): before = lax.ppermute(last, axis, up)  8.63 us
    all_to_all x1, waiting for transfers between devices, reciprocal(): lax.all_to_all(imag_part, ('gx', 'gz'), split_axis=1, concat_axis=0, tile...  6.82 us
    all_to_all x1, waiting for transfers between devices, reciprocal(): lax.all_to_all(out_imag, ('gx', 'gz'), split_axis=0, concat_axis=1, tiled...  6.6 us
  transfers between devices with their start and end apart: 28, of which 22 were waited for; matrix products, arithmetic and copies ran while one was open for 9% of the time, Pallas kernels for 0%

commit v1 on v0

v1 whole, which is shorter than its diff:
```python
import functools
import math

import jax
import jax.numpy as jnp
from jax import lax
from jax.experimental import pallas as pl
from jax.experimental.pallas import tpu as pltpu
from jax.sharding import PartitionSpec as P

PC = 16
LANES = 128
pair_scale = 0.1
coupling = 0.125
spread_width = 0.0625
highest = lax.Precision.HIGHEST
AXES = ("gx", "gy", "gz")
f32 = jnp.float32
bf16 = jnp.bfloat16
NT = (((1,), (1,)), ((), ()))
TN = (((0,), (0,)), ((), ()))


def full_spec(shape):
    return pl.BlockSpec(shape, lambda *_: (0,) * len(shape))


def cell_spec(shape):
    return pl.BlockSpec((1,) + tuple(shape[1:]), lambda i: (i,) + (0,) * (len(shape) - 1))


def split3(value):
    hi = lax.reduce_precision(value, 8, 7)
    rest = value - hi
    mid = lax.reduce_precision(rest, 8, 7)
    return hi, mid, rest - mid


def cas(first, second, length):
    angle = 2.0 * math.pi / length * (first[:, None] * second[None, :] % length).astype(f32)
    return jnp.cos(angle) + jnp.sin(angle)


def offsets():
    return [(i, j, k) for i in (-1, 0, 1) for j in (-1, 0, 1) for k in (-1, 0, 1)]


def offset_table():
    rows = []
    for o in offsets():
        norm = float(o[0] ** 2 + o[1] ** 2 + o[2] ** 2)
        doubled = [2.0 * v for v in o]
        rows.append([1.0] * 6 + doubled + [1.0] * 3 + [-v for v in doubled] + [-norm])
    return jnp.broadcast_to(jnp.array(rows, f32)[:, :, None], (27, 16, LANES)).astype(bf16)


def slot(offset, devices, length):
    if devices == 2 and length == 1:
        return 0 if offset == 0 else 1
    return 1 + offset


def with_halo(shard, axis, dim):
    devices, length = lax.axis_size(axis), shard.shape[dim]
    up = [(i, (i + 1) % devices) for i in range(devices)]
    down = [(j, i) for i, j in up]
    if devices == 2 and length == 1:
        return jnp.concatenate([shard, lax.ppermute(shard, axis, up)], axis=dim)
    last = lax.slice_in_dim(shard, length - 1, length, axis=dim)
    first = lax.slice_in_dim(shard, 0, 1, axis=dim)
    before = lax.ppermute(last, axis, up)
    after = lax.ppermute(first, axis, down)
    return jnp.concatenate([before, shard, after], axis=dim)


def exchange_halo(shard):
    shard = with_halo(shard, "gy", 1)
    shard = with_halo(shard, "gx", 0)
    return with_halo(shard, "gz", 2)


def pair_total(cells, counts, centre, table_ref, near_ref, value_ref):
    index = pl.program_id(0)
    at_z = index % cells[2]
    at_y = index // cells[2] % cells[1]
    at_x = index // (cells[2] * cells[1])
    total = jnp.zeros((centre.shape[1], value_ref.shape[-1]), f32)
    for which, o in enumerate(offsets()):
        where = [
            base + slot(step, count, length)
            for base, step, count, length in zip((at_x, at_y, at_z), o, counts, cells)
        ]
        near = near_ref[where[0], where[1], where[2]] * table_ref[which]
        inside = lax.dot_general(centre, near, TN, preferred_element_type=f32)
        inside = jnp.maximum(inside, 0.0)
        weight = (pair_scale * inside * inside).astype(bf16)
        total = total + jnp.dot(
            weight, value_ref[where[0], where[1], where[2]], preferred_element_type=f32
        )
    return total


def message_kernel(
    cells, counts, centre_ref, table_ref, near_ref, value_ref, feature_ref, self_ref, read_ref, pre_ref, charge_ref
):
    message = pair_total(cells, counts, centre_ref[0], table_ref, near_ref, value_ref)
    preact = jnp.dot(feature_ref[0], self_ref[...], preferred_element_type=f32) + message
    pre_ref[0] = preact
    active = preact / (1.0 + jnp.exp(-preact))
    charge_ref[0] = lax.dot_general(
        read_ref[...], active, NT, precision=highest, preferred_element_type=f32
    )


def back_kernel(
    cells, counts, centre_ref, table_ref, near_ref, value_ref, cot_ref, msg_ref, self_ref, out_ref
):
    total = pair_total(cells, counts, centre_ref[0], table_ref, near_ref, value_ref)
    grad = lax.dot_general(total.astype(bf16), msg_ref[...], NT, preferred_element_type=f32)
    out_ref[0] = grad + lax.dot_general(
        cot_ref[0], self_ref[...], NT, preferred_element_type=f32
    )


def spline(corner, fraction, points, start=0):
    atoms = corner.shape[-1]
    offset = lax.broadcasted_iota(jnp.int32, (points, atoms), 0) - start - corner
    u = fraction
    first = (1.0 - u) * (1.0 - u) * (1.0 - u) / 6.0
    second = (3.0 * u * u * u - 6.0 * u * u + 4.0) / 6.0
    third = (-3.0 * u * u * u + 3.0 * u * u + 3.0 * u + 1.0) / 6.0
    fourth = u * u * u / 6.0
    zero = jnp.zeros((points, atoms), f32)
    return jnp.where(
        offset == 0,
        first,
        jnp.where(offset == 1, second, jnp.where(offset == 2, third, jnp.where(offset == 3, fourth, zero))),
    )


def spread_kernel(dims, corner_ref, fraction_ref, charge_ref, wave_ref, out_ref, hx_ref, left_ref):
    local_x, local_y, local_z, pack = dims
    rows_x = spline(corner_ref[0:1, :], fraction_ref[0:1, :], local_x)
    rows_y = spline(corner_ref[1:2, :], fraction_ref[1:2, :], local_y)
    hx_ref[...] = charge_ref[...] * jnp.dot(
        wave_ref[...], rows_x, precision=highest, preferred_element_type=f32
    )
    half = hx_ref.shape[0] // pack
    total = None
    for h in range(pack):

        def fill(k, carry):
            left_ref[pl.ds(pl.multiple_of(k * local_y, local_y), local_y), :] = (
                hx_ref[pl.ds(h * half + k, 1), :] * rows_y
            ).astype(bf16)
            return carry

        lax.fori_loop(0, half, fill, 0, unroll=8)
        right = spline(corner_ref[2:3, :], fraction_ref[2:3, :], LANES, h * local_z).astype(bf16)
        part = lax.dot_general(left_ref[...], right, NT, preferred_element_type=f32)
        total = part if total is None else total + part
    out_ref[...] = total.astype(bf16)


def plane_kernel(dims, count_x, got_ref, z_ref, y_ref, g_ref, out_ref):
    count_y, count_z, pack = dims
    rows = got_ref.shape[1]
    each = count_y * count_z
    halves = [None] * pack
    for c in range(count_z):
        stack = []
        for b in range(count_y):
            block = got_ref[b * count_z + c].astype(f32)
            for a in range(1, count_x):
                block = block + got_ref[a * each + b * count_z + c].astype(f32)
            stack.append(block)
        stack = jnp.concatenate(stack, axis=0)
        for h in range(pack):
            part = jnp.dot(stack, z_ref[c, h], precision=highest, preferred_element_type=f32)
            halves[h] = part if halves[h] is None else halves[h] + part
    lines = jnp.concatenate(halves, axis=0)
    wave = jnp.dot(y_ref[...], lines, precision=highest, preferred_element_type=f32)
    scaled = g_ref[...] * wave
    energy = jnp.sum(jnp.sum(scaled * wave, axis=1, keepdims=True), axis=0, keepdims=True)
    hi = energy.astype(bf16).astype(f32)
    mid = (energy - hi).astype(bf16).astype(f32)
    low = energy - hi - mid
    which = lax.broadcasted_iota(jnp.int32, (16, LANES), 0)
    tail = jnp.where(which == 0, hi, jnp.where(which == 1, mid, jnp.where(which == 2, low, 0.0)))
    back = lax.dot_general(y_ref[...], scaled, TN, precision=highest, preferred_element_type=f32)
    high = back.shape[0] // pack
    for c in range(count_z):
        total = None
        for h in range(pack):
            part = lax.dot_general(
                back[h * high : (h + 1) * high], z_ref[c, h], NT, precision=highest, preferred_element_type=f32
            )
            total = part if total is None else total + part
        for b in range(count_y):
            out_ref[b * count_z + c, 0:rows, :] = total[b * rows : (b + 1) * rows].astype(bf16)
            out_ref[b * count_z + c, rows : rows + 16, :] = tail.astype(bf16)


def field_kernel(dims, scale, escale, owners, corner_ref, fraction_ref, wave_ref, got_ref, out_ref, energy_ref, hx_ref):
    local_x, local_y, local_z, pack, rows = dims
    atoms = corner_ref.shape[-1]
    rows_x = spline(corner_ref[0:1, :], fraction_ref[0:1, :], local_x)
    rows_y = spline(corner_ref[1:2, :], fraction_ref[1:2, :], local_y)
    hx_ref[...] = jnp.dot(wave_ref[...], rows_x, precision=highest, preferred_element_type=f32)
    half = hx_ref.shape[0] // pack
    per = rows // local_y
    acc = jnp.zeros((local_y, atoms), f32)
    for h in range(pack):
        right = spline(corner_ref[2:3, :], fraction_ref[2:3, :], LANES, h * local_z).astype(bf16)

        def step(q, acc):
            block = got_ref[q, 0:rows, :]
            value = jnp.dot(block, right, preferred_element_type=f32)
            for k in range(per):
                acc = acc + value[k * local_y : (k + 1) * local_y] * hx_ref[
                    pl.ds(h * half + q * per + k, 1), :
                ]
            return acc

        acc = lax.fori_loop(0, owners, step, acc, unroll=4)
    value = scale * jnp.sum(acc * rows_y, axis=0, keepdims=True)
    out_ref[...] = jnp.broadcast_to(value, out_ref.shape)
    tail = jnp.zeros((16, LANES), f32)
    for q in range(owners):
        tail = tail + got_ref[q, rows : rows + 16, :].astype(f32)
    energy_ref[...] = jnp.broadcast_to(escale * jnp.sum(tail, axis=0, keepdims=True), energy_ref.shape)


def influence_of(index_x, index_y, index_z, size_x, size_y, size_z, points):
    def wave(index, size):
        signed = jnp.where(2 * index >= size, index - size, index)
        return signed.astype(f32) * (points / size)

    wave_x = wave(index_x, size_x)
    wave_y = wave(index_y, size_y)
    wave_z = wave(index_z, size_z)
    squared = wave_x * wave_x + wave_y * wave_y + wave_z * wave_z
    safe = jnp.where(squared > 0, squared, 1.0)
    return jnp.where(squared > 0, jnp.exp(-((math.pi * spread_width) ** 2) * squared) / safe, 0.0)


def exchange_planes(payload):
    return lax.all_to_all(payload, AXES, split_axis=0, concat_axis=0, tiled=True)


def params(**kw):
    return pltpu.CompilerParams(vmem_limit_bytes=48 * 1024 * 1024, **kw)


def body(features, msg_weight, self_weight, charge_weight, spline_corner, spline_fraction):
    cells = features.shape[:3]
    slots, width = features.shape[3:]
    number = cells[0] * cells[1] * cells[2]
    counts = tuple(lax.axis_size(a) for a in AXES)
    devices = counts[0] * counts[1] * counts[2]
    local = tuple(c * PC for c in cells)
    size = tuple(c * n for c, n in zip(local, counts))
    pack = LANES // local[2]
    planes = max(pack, size[0] // devices)
    owners = size[0] // planes
    inner = planes // pack
    rows = inner * local[1]
    atoms = number * slots
    volume = size[0] // PC * (size[1] // PC) * (size[2] // PC)

    flat = features.reshape(number * slots, width)
    projected = jnp.dot(flat, msg_weight, preferred_element_type=f32).astype(bf16).reshape(features.shape)
    position = lax.reduce_precision(
        (spline_corner.astype(f32) + 1.0 + spline_fraction) / PC, 8, 7
    )
    norm = jnp.sum(position * position, axis=3, keepdims=True)
    one = jnp.ones_like(norm)
    near = jnp.concatenate(
        [position, one, one, one, one, one, one, *split3(-norm), position, one], axis=3
    ).astype(bf16)
    centre = jnp.concatenate(
        [2.0 * position, *split3(1.0 - norm), position] + [one] * 7, axis=3
    ).astype(bf16).reshape(number, 16, slots)
    table = offset_table()

    padded = exchange_halo(jnp.concatenate([projected, near], axis=3))
    values = padded[:, :, :, :slots]
    nears = padded[:, :, :, slots:]

    read = jnp.broadcast_to(charge_weight.astype(f32)[None, :], (8, width))
    cell_features = features.reshape(number, slots, width)
    square = (number, slots, width)
    preact, charge = pl.pallas_call(
        functools.partial(message_kernel, cells, counts),
        out_shape=(jax.ShapeDtypeStruct(square, f32), jax.ShapeDtypeStruct((number, 8, slots), f32)),
        grid=(number,),
        in_specs=[
            cell_spec(centre.shape),
            full_spec(table.shape),
            full_spec(nears.shape),
            full_spec(values.shape),
            cell_spec(square),
            full_spec(self_weight.shape),
            full_spec(read.shape),
        ],
        out_specs=(cell_spec(square), cell_spec((number, 8, slots))),
        compiler_params=params(),
        name="message",
    )(centre, table, nears, values, cell_features, self_weight, read)

    shift = jnp.stack(
        [lax.broadcasted_iota(jnp.int32, cells + (slots,), d) * PC for d in range(3)], axis=0
    )
    corner = (spline_corner.transpose(3, 0, 1, 2, 4) + shift).reshape(3, atoms)
    fraction = spline_fraction.transpose(3, 0, 1, 2, 4).reshape(3, atoms)
    order = (
        jnp.arange(pack, dtype=jnp.int32)[:, None, None] * inner
        + jnp.arange(owners, dtype=jnp.int32)[None, :, None] * planes
        + jnp.arange(inner, dtype=jnp.int32)[None, None, :]
    ).reshape(-1)
    here = lax.axis_index("gx") * local[0] + jnp.arange(local[0], dtype=jnp.int32)
    wave_x = cas(order, here, size[0])
    charges = charge[:, 0, :].reshape(1, atoms)
    payload = pl.pallas_call(
        functools.partial(spread_kernel, (local[0], local[1], local[2], pack)),
        out_shape=jax.ShapeDtypeStruct((owners * rows, LANES), bf16),
        scratch_shapes=[
            pltpu.VMEM((size[0], atoms), f32),
            pltpu.VMEM((owners * rows, atoms), bf16),
        ],
        compiler_params=params(),
        name="spread",
    )(corner, fraction, charges, wave_x).reshape(owners, rows, LANES)
    if owners < devices:
        payload = jnp.pad(payload, ((0, devices - owners), (0, 0), (0, 0)))
    got = exchange_planes(payload)

    range_y = jnp.arange(size[1], dtype=jnp.int32)
    range_z = jnp.arange(size[2], dtype=jnp.int32)
    cas_z = cas(range_z, range_z, size[2]).reshape(counts[2], 1, local[2], size[2])
    blank = jnp.zeros_like(cas_z)
    wide_z = jnp.concatenate(
        [
            jnp.concatenate([cas_z if at == h else blank for at in range(pack)], axis=2)
            for h in range(pack)
        ],
        axis=1,
    )
    cas_y = cas(range_y, range_y, size[1]).reshape(size[1], counts[1], local[1])
    same = jnp.eye(planes, dtype=f32).reshape(pack, inner, pack, inner)
    wide_y = jnp.einsum("abcd,kgy->abkcgdy", same, cas_y, precision=highest).reshape(
        planes * size[1], planes * size[1]
    )
    me = lax.axis_index(AXES)
    index_x = me * planes + jnp.arange(planes, dtype=jnp.int32)
    influence = influence_of(
        index_x[:, None, None], range_y[None, :, None], range_z[None, None, :], *size, PC
    ).reshape(planes * size[1], size[2])
    each = counts[1] * counts[2]
    solved = pl.pallas_call(
        functools.partial(plane_kernel, (counts[1], counts[2], pack), counts[0]),
        out_shape=jax.ShapeDtypeStruct((each, rows + 16, LANES), bf16),
        compiler_params=params(),
        name="planes",
    )(got, wide_z, wide_y, influence)
    field = exchange_planes(jnp.tile(solved, (counts[0], 1, 1)))

    potential, energy = pl.pallas_call(
        functools.partial(
            field_kernel,
            (local[0], local[1], local[2], pack, rows),
            coupling / volume,
            coupling / (2.0 * volume * atoms * devices),
            owners,
        ),
        out_shape=(jax.ShapeDtypeStruct((8, atoms), f32), jax.ShapeDtypeStruct((8, LANES), f32)),
        scratch_shapes=[pltpu.VMEM((size[0], atoms), f32)],
        compiler_params=params(),
        name="field",
    )(corner, fraction, wave_x, field)
    potential = potential[0].reshape(cells + (slots,))

    pre = preact.reshape(features.shape)
    sigma = jax.nn.sigmoid(pre)
    slope = sigma * (1.0 + pre * (1.0 - sigma))
    cotangent = (potential[..., None] * charge_weight.astype(f32) * slope).astype(bf16)
    cots = exchange_halo(cotangent)
    grad = pl.pallas_call(
        functools.partial(back_kernel, cells, counts),
        out_shape=jax.ShapeDtypeStruct(square, f32),
        grid=(number,),
        in_specs=[
            cell_spec(centre.shape),
            full_spec(table.shape),
            full_spec(nears.shape),
            full_spec(cots.shape),
            cell_spec(square),
            full_spec(msg_weight.shape),
            full_spec(self_weight.shape),
        ],
        out_specs=cell_spec(square),
        compiler_params=params(),
        name="back",
    )(centre, table, nears, cots, cotangent.reshape(square), msg_weight, self_weight)
    return (grad.reshape(features.shape), potential, energy[0, 0])


def solution(mesh):
    split = P("gx", "gy", "gz", None, None)
    in_specs = (split, P(), P(), P(), split, split)
    out_specs = (split, P("gx", "gy", "gz", None), P())
    return jax.shard_map(body, mesh=mesh, in_specs=in_specs, out_specs=out_specs, check_vma=False)
```

time: 314 us -> 133 us (0.42); the launches traced: 309 us -> 132 us
  matrix products: 62.1 us -> 1.16 us
  waiting for transfers between devices: 113 us -> 69.8 us
  blocking collectives: 39.9 us -> 0 us
  starting transfers between devices: 59.2 us -> 22.5 us
  Pallas kernels: 0 us -> 28.1 us
  local copies, waits for them, and re-layouts: 22.5 us -> 4.47 us
  other arithmetic: 9.17 us -> 4.96 us
    dot_general x80 -> x1, matrix products: 62.1 us -> 1.16 us  [body(): jnp.dot(flat, msg_weight, preferred_element_type=f32).astype(bf16)]
    psum x1 -> x0, blocking collectives: 39.9 us -> none  [reciprocal(): total = lax.psum(energy_part, ('gx', 'gy', 'gz'))]
    pallas_call x0 -> x5, Pallas kernels: none -> 28.1 us  [the longest x1 8.21 us: body(): pl.pallas_call(functools.partial(message_kernel, cells, counts), out_shap...]
    all_to_all x10 -> x2, starting transfers between devices: 34.8 us -> 7.15 us  [exchange_planes(): lax.all_to_all(payload, AXES, split_axis=0, concat_axis=0, tiled=True)]
    all_to_all x10 -> x2, waiting for transfers between devices: 42.5 us -> 23.2 us  [exchange_planes(): lax.all_to_all(payload, AXES, split_axis=0, concat_axis=0, tiled=True)]
    ppermute x9 -> x4, waiting for transfers between devices: 36.7 us -> 24.6 us  [with_halo(): before = lax.ppermute(last, axis, up)]
    ppermute x9 -> x6, waiting for transfers between devices: 33.8 us -> 22 us  [the longest x2 11.6 us: with_halo(): return jnp.concatenate([shard, lax.ppermute(shard, axis, up)], axis=dim)]
    ppermute x9 -> x4, starting transfers between devices: 8.63 us -> 1.8 us  [with_halo(): before = lax.ppermute(last, axis, up)]
  transfers between devices with their start and end apart: 28 -> 12, of which waited for: 22 -> 11; matrix products, arithmetic and copies ran while one was open for 9% -> 4% of each run, Pallas kernels for 0% -> 0%
where the time goes in v1:
time: 133 us; the launch traced here: 132 us
  waiting for transfers between devices  69.8 us (52%)
  Pallas kernels  28.1 us (21%)
  starting transfers between devices  22.5 us (17%)
  other arithmetic  4.96 us (4%)
  local copies, waits for them, and re-layouts  4.47 us (3%)
    ppermute x4, waiting for transfers between devices, with_halo(): before = lax.ppermute(last, axis, up)  24.6 us
    all_to_all x2, waiting for transfers between devices, exchange_planes(): lax.all_to_all(payload, AXES, split_axis=0, concat_axis=0, tiled=True)  23.2 us
    ppermute x2, waiting for transfers between devices, with_halo(): return jnp.concatenate([shard, lax.ppermute(shard, axis, up)], axis=dim)  11.6 us
    ppermute x4, waiting for transfers between devices, with_halo(): after = lax.ppermute(first, axis, down)  10.4 us
    ppermute x4, starting transfers between devices, with_halo(): after = lax.ppermute(first, axis, down)  9.53 us
    pallas_call x1, Pallas kernels, body(): pl.pallas_call(functools.partial(message_kernel, cells, counts), out_shap...  8.21 us
    pallas_call x1, Pallas kernels, body(): pl.pallas_call(functools.partial(back_kernel, cells, counts), out_shape=j...  8 us
    all_to_all x2, starting transfers between devices, exchange_planes(): lax.all_to_all(payload, AXES, split_axis=0, concat_axis=0, tiled=True)  7.15 us
  transfers between devices with their start and end apart: 12, of which 11 were waited for; matrix products, arithmetic and copies ran while one was open for 4% of the time, Pallas kernels for 0%

profile of v1, /device:TPU:0, one launch (start us, length us, event | category | flops | bytes accessed | tf_op | source)
XLA Modules:
  0.0 132.0 jit_solution(5114080841966065186)
XLA Ops:
  2.9 3.0 %collective-permute-start = (bf16[2,1,4,144,128]{4,3,2,1,0:T(8,128)(2,1)S(1)}, bf16[2,1,4,144,128]{4,3,2,1,0:T(8,128)(2,1)S(1)}, u32[]{:S(2)}, u32[]{:S(2)}) collective-permute-start(bf16[2,1,4,144,128]{4,3,2,1,0:T(8,128)(2,1)S(1)} %concatenate.75), channel_id=1, source_target_pairs={{0,4},{4,0},{1,5},{5,1},{2,6},{6,2},{3,7},{7,3},{8,12},{12,8},{9,1... | collective-permute-start | bytes 884744 | tf_op jit(solution)/shard_map/ppermute | solution.py:68
  8.9 4.1 %collective-permute-done = bf16[2,1,4,144,128]{4,3,2,1,0:T(8,128)(2,1)S(1)} collective-permute-done((bf16[2,1,4,144,128]{4,3,2,1,0:T(8,128)(2,1)S(1)}, bf16[2,1,4,144,128]{4,3,2,1,0:T(8,128)(2,1)S(1)}, u32[]{:S(2)}, u32[]{:S(2)}) %collective-permute-start) | collective-permute-done | bytes 294944 | tf_op jit(solution)/shard_map/ppermute | solution.py:68
  13.1 1.7 %collective-permute-start.2 = (bf16[1,2,4,144,128]{4,3,2,1,0:T(8,128)(2,1)S(1)}, bf16[1,2,4,144,128]{4,3,2,1,0:T(8,128)(2,1)S(1)}, u32[]{:S(2)}, u32[]{:S(2)}) collective-permute-start(bf16[1,2,4,144,128]{4,3,2,1,0:T(8,128)(2,1)S(1)} %get-tuple-element.31), channel_id=1, source_target_pairs={{8,0},{16,8},{24,16},{0,24},{9,1},{17,9},{25,17},{1,25},{10,2},{18... | collective-permute-start | bytes 884744 | tf_op jit(solution)/shard_map/ppermute | solution.py:72
  16.0 4.4 %collective-permute-done.1 = bf16[1,2,4,144,128]{4,3,2,1,0:T(8,128)(2,1)S(1)} collective-permute-done((bf16[1,2,4,144,128]{4,3,2,1,0:T(8,128)(2,1)S(1)}, bf16[1,2,4,144,128]{4,3,2,1,0:T(8,128)(2,1)S(1)}, u32[]{:S(2)}, u32[]{:S(2)}) %collective-permute-start.1) | collective-permute-done | bytes 294944 | tf_op jit(solution)/shard_map/ppermute | solution.py:71
  20.3 1.3 %collective-permute-done.2 = bf16[1,2,4,144,128]{4,3,2,1,0:T(8,128)(2,1)S(1)} collective-permute-done((bf16[1,2,4,144,128]{4,3,2,1,0:T(8,128)(2,1)S(1)}, bf16[1,2,4,144,128]{4,3,2,1,0:T(8,128)(2,1)S(1)}, u32[]{:S(2)}, u32[]{:S(2)}) %collective-permute-start.2) | collective-permute-done | bytes 294944 | tf_op jit(solution)/shard_map/ppermute | solution.py:72
  21.8 1.6 %collective-permute-start.3 = (bf16[4,2,1,144,128]{4,3,2,1,0:T(8,128)(2,1)S(1)}, bf16[4,2,1,144,128]{4,3,2,1,0:T(8,128)(2,1)S(1)}, u32[]{:S(2)}, u32[]{:S(2)}) collective-permute-start(bf16[4,2,1,144,128]{4,3,2,1,0:T(8,128)(2,1)S(1)} %get-tuple-element.26), channel_id=1, source_target_pairs={{0,1},{1,2},{2,3},{3,0},{4,5},{5,6},{6,7},{7,4},{8,9},{9,10},{10,1... | collective-permute-start | bytes 884744 | tf_op jit(solution)/shard_map/ppermute | solution.py:71
  23.4 2.3 %collective-permute-start.4 = (bf16[4,2,1,144,128]{4,3,2,1,0:T(8,128)(2,1)S(1)}, bf16[4,2,1,144,128]{4,3,2,1,0:T(8,128)(2,1)S(1)}, u32[]{:S(2)}, u32[]{:S(2)}) collective-permute-start(bf16[4,2,1,144,128]{4,3,2,1,0:T(8,128)(2,1)S(1)} %get-tuple-element.27), channel_id=1, source_target_pairs={{1,0},{2,1},{3,2},{0,3},{5,4},{6,5},{7,6},{4,7},{9,8},{10,9},{11,1... | collective-permute-start | bytes 884744 | tf_op jit(solution)/shard_map/ppermute | solution.py:72
  25.8 7.8 %collective-permute-done.3 = bf16[4,2,1,144,128]{4,3,2,1,0:T(8,128)(2,1)S(1)} collective-permute-done((bf16[4,2,1,144,128]{4,3,2,1,0:T(8,128)(2,1)S(1)}, bf16[4,2,1,144,128]{4,3,2,1,0:T(8,128)(2,1)S(1)}, u32[]{:S(2)}, u32[]{:S(2)}) %collective-permute-start.3) | collective-permute-done | bytes 294944 | tf_op jit(solution)/shard_map/ppermute | solution.py:71
  33.5 5.6 %collective-permute-done.4 = bf16[4,2,1,144,128]{4,3,2,1,0:T(8,128)(2,1)S(1)} collective-permute-done((bf16[4,2,1,144,128]{4,3,2,1,0:T(8,128)(2,1)S(1)}, bf16[4,2,1,144,128]{4,3,2,1,0:T(8,128)(2,1)S(1)}, u32[]{:S(2)}, u32[]{:S(2)}) %collective-permute-start.4) | collective-permute-done | bytes 294944 | tf_op jit(solution)/shard_map/ppermute | solution.py:72
  40.3 8.2 %message.1 = (f32[8,128,128]{2,1,0:T(8,128)S(1)}, f32[8,8,128]{2,1,0:T(8,128)S(1)}) custom-call(bf16[8,16,128]{2,1,0:T(8,128)(2,1)S(1)} %concatenate.69.centre_ref, bf16[27,16,128]{2,1,0:T(8,128)(2,1)S(1)} %broadcast_in_dim.8.table_ref, bf16[4,2,6,16,128]{4,3,2,1,0:T(8,128)(2,1)S(1)} %pad_maximum_fusion.16.near_ref, ...), custom_call_target="tpu_custom_call" | custom-call | tf_op jit(solution)/shard_map/message/pallas_call | solution.py:293
  48.5 3.9 %spread.1 = bf16[1024,128]{1,0:T(8,128)(2,1)} custom-call(s32[3,1024]{1,0:T(4,128)S(1)} %reshape.568.corner_ref, f32[3,1024]{1,0:T(4,128)S(1)} %reshape.569.fraction_ref, f32[1,1024]{1,0:T(1,128)S(1)} %slice_bitcast_fusion.charge_ref, f32[128,32]{1,0:T(8,128)S(1)} %sine_add_fusion.1.wave_ref), custom_call_target="tpu_custom_call" | custom-call | tf_op jit(solution)/shard_map/spread/pallas_call | solution.py:324
  52.4 4.6 %all-to-all-start = ((bf16[32,32,128]{2,1,0:T(8,128)(2,1)}), bf16[32,32,128]{2,1,0:T(8,128)(2,1)S(1)}, u32[]{:S(2)}, u32[]{:S(2)}) async-start(bf16[32,32,128]{2,1,0:T(8,128)(2,1)} %bitcast.13), calls=%async_computation | async-start | bytes 524288 | tf_op jit(solution)/shard_map/all_to_all | solution.py:248
  57.8 9.9 %all-to-all-done.got_ref = bf16[32,32,128]{2,1,0:T(8,128)(2,1)S(1)} async-done(((bf16[32,32,128]{2,1,0:T(8,128)(2,1)}), bf16[32,32,128]{2,1,0:T(8,128)(2,1)S(1)}, u32[]{:S(2)}, u32[]{:S(2)}) %all-to-all-start) | async-done | bytes 262176 | tf_op jit(solution)/shard_map/all_to_all | solution.py:248
  67.7 2.4 %planes.1 = bf16[8,48,128]{2,1,0:T(8,128)(2,1)S(1)} custom-call(bf16[32,32,128]{2,1,0:T(8,128)(2,1)S(1)} %all-to-all-done.got_ref, f32[4,2,128,256]{3,2,1,0:T(8,128)S(1)} %select_maximum_fusion.z_ref, f32[128,128]{1,0:T(8,128)S(1)} %copy.59.y_ref, f32[128,256]{1,0:T(8,128)S(1)} %fusion.8.g_ref), custom_call_target="tpu_custom_call" | custom-call | tf_op jit(solution)/shard_map/planes/pallas_call | solution.py:360
  71.0 2.6 %all-to-all-start.1 = ((bf16[32,48,128]{2,1,0:T(8,128)(2,1)}), bf16[32,48,128]{2,1,0:T(8,128)(2,1)S(1)}, u32[]{:S(2)}, u32[]{:S(2)}) async-start(bf16[32,48,128]{2,1,0:T(8,128)(2,1)} %bitcast.15), calls=%async_computation.1 | async-start | bytes 786432 | tf_op jit(solution)/shard_map/all_to_all | solution.py:248
  73.6 13.2 %all-to-all-done.1.got_ref = bf16[32,48,128]{2,1,0:T(8,128)(2,1)S(1)} async-done(((bf16[32,48,128]{2,1,0:T(8,128)(2,1)}), bf16[32,48,128]{2,1,0:T(8,128)(2,1)S(1)}, u32[]{:S(2)}, u32[]{:S(2)}) %all-to-all-start.1) | async-done | bytes 393248 | tf_op jit(solution)/shard_map/all_to_all | solution.py:248
  86.8 5.6 %field.1 = (f32[8,1024]{1,0:T(8,128)S(1)}, f32[8,128]{1,0:T(8,128)S(1)}) custom-call(s32[3,1024]{1,0:T(4,128)S(1)} %reshape.568.corner_ref, f32[3,1024]{1,0:T(4,128)S(1)} %reshape.569.fraction_ref, f32[128,32]{1,0:T(8,128)S(1)} %sine_add_fusion.1.wave_ref, bf16[32,48,128]{2,1,0:T(8,128)(2,1)S(1)} %all-to-all-done.1.got_ref), custom_call_target="tpu_custom_call" | custom-call | tf_op jit(solution)/shard_map/field/pallas_call | solution.py:368
  93.7 7.5 %collective-permute-done.5 = bf16[2,1,4,128,128]{4,3,2,1,0:T(8,128)(2,1)S(1)} collective-permute-done((bf16[2,1,4,128,128]{4,3,2,1,0:T(8,128)(2,1)S(1)}, bf16[2,1,4,128,128]{4,3,2,1,0:T(8,128)(2,1)S(1)}, u32[]{:S(2)}, u32[]{:S(2)}) %collective-permute-start.5) | collective-permute-done | bytes 262176 | tf_op jit(solution)/shard_map/ppermute | solution.py:68
  101.3 1.7 %collective-permute-start.7 = (bf16[1,2,4,128,128]{4,3,2,1,0:T(8,128)(2,1)S(1)}, bf16[1,2,4,128,128]{4,3,2,1,0:T(8,128)(2,1)S(1)}, u32[]{:S(2)}, u32[]{:S(2)}) collective-permute-start(bf16[1,2,4,128,128]{4,3,2,1,0:T(8,128)(2,1)S(1)} %get-tuple-element.33), channel_id=1, source_target_pairs={{8,0},{16,8},{24,16},{0,24},{9,1},{17,9},{25,17},{1,25},{10,2},{18... | collective-permute-start | bytes 786440 | tf_op jit(solution)/shard_map/ppermute | solution.py:72
  103.0 6.0 %collective-permute-done.6 = bf16[1,2,4,128,128]{4,3,2,1,0:T(8,128)(2,1)S(1)} collective-permute-done((bf16[1,2,4,128,128]{4,3,2,1,0:T(8,128)(2,1)S(1)}, bf16[1,2,4,128,128]{4,3,2,1,0:T(8,128)(2,1)S(1)}, u32[]{:S(2)}, u32[]{:S(2)}) %collective-permute-start.6) | collective-permute-done | bytes 262176 | tf_op jit(solution)/shard_map/ppermute | solution.py:71
  109.2 3.8 %collective-permute-start.9 = (bf16[4,2,1,128,128]{4,3,2,1,0:T(8,128)(2,1)S(1)}, bf16[4,2,1,128,128]{4,3,2,1,0:T(8,128)(2,1)S(1)}, u32[]{:S(2)}, u32[]{:S(2)}) collective-permute-start(bf16[4,2,1,128,128]{4,3,2,1,0:T(8,128)(2,1)S(1)} %get-tuple-element.29), channel_id=1, source_target_pairs={{1,0},{2,1},{3,2},{0,3},{5,4},{6,5},{7,6},{4,7},{9,8},{10,9},{11,1... | collective-permute-start | bytes 786440 | tf_op jit(solution)/shard_map/ppermute | solution.py:72
  113.7 6.4 %collective-permute-done.8 = bf16[4,2,1,128,128]{4,3,2,1,0:T(8,128)(2,1)S(1)} collective-permute-done((bf16[4,2,1,128,128]{4,3,2,1,0:T(8,128)(2,1)S(1)}, bf16[4,2,1,128,128]{4,3,2,1,0:T(8,128)(2,1)S(1)}, u32[]{:S(2)}, u32[]{:S(2)}) %collective-permute-start.8) | collective-permute-done | bytes 262176 | tf_op jit(solution)/shard_map/ppermute | solution.py:71
  120.2 3.5 %collective-permute-done.9 = bf16[4,2,1,128,128]{4,3,2,1,0:T(8,128)(2,1)S(1)} collective-permute-done((bf16[4,2,1,128,128]{4,3,2,1,0:T(8,128)(2,1)S(1)}, bf16[4,2,1,128,128]{4,3,2,1,0:T(8,128)(2,1)S(1)}, u32[]{:S(2)}, u32[]{:S(2)}) %collective-permute-start.9) | collective-permute-done | bytes 262176 | tf_op jit(solution)/shard_map/ppermute | solution.py:72
  124.0 8.0 %back.1 = f32[8,128,128]{2,1,0:T(8,128)} custom-call(bf16[8,16,128]{2,1,0:T(8,128)(2,1)S(1)} %concatenate.69.centre_ref, bf16[27,16,128]{2,1,0:T(8,128)(2,1)S(1)} %broadcast_in_dim.8.table_ref, bf16[4,2,6,16,128]{4,3,2,1,0:T(8,128)(2,1)S(1)} %pad_maximum_fusion.16.near_ref, bf16[4,2,6,128,128]{4,3,2,1,0:T(8,128)(2,1)S(1)} %pad_maximum_fusion.5.value_ref, ...), custom_call_target="tpu_custom_call" | custom-call | tf_op jit(solution)/shard_map/back/pallas_call | solution.py:388
  (82 shorter events, 11.7 us)
Async XLA Ops:
  2.9 10.0 %collective-permute-start = (bf16[2,1,4,144,128]{4,3,2,1,0:T(8,128)(2,1)S(1)}, bf16[2,1,4,144,128]{4,3,2,1,0:T(8,128)(2,1)S(1)}, u32[]{:S(2)}, u32[]{:S(2)}) collective-permute-start(bf16[2,1,4,144,128]{4,3,2,1,0:T(8,128)(2,1)S(1)} %concatenate.75), channel_id=1, source_target_pairs={{0,4},{4,0},{1,5},{5,1},{2,6},{6,2},{3,7},{7,3},{8,12},{12,8},{9,1... | collective-permute-start | bytes 884744 | tf_op jit(solution)/shard_map/ppermute | solution.py:68
  13.0 7.3 %collective-permute-start.1 = (bf16[1,2,4,144,128]{4,3,2,1,0:T(8,128)(2,1)S(1)}, bf16[1,2,4,144,128]{4,3,2,1,0:T(8,128)(2,1)S(1)}, u32[]{:S(2)}, u32[]{:S(2)}) collective-permute-start(bf16[1,2,4,144,128]{4,3,2,1,0:T(8,128)(2,1)S(1)} %get-tuple-element.30), channel_id=1, source_target_pairs={{0,8},{8,16},{16,24},{24,0},{1,9},{9,17},{17,25},{25,1},{2,10},{10... | collective-permute-start | bytes 884744 | tf_op jit(solution)/shard_map/ppermute | solution.py:71
  13.1 8.6 %collective-permute-start.2 = (bf16[1,2,4,144,128]{4,3,2,1,0:T(8,128)(2,1)S(1)}, bf16[1,2,4,144,128]{4,3,2,1,0:T(8,128)(2,1)S(1)}, u32[]{:S(2)}, u32[]{:S(2)}) collective-permute-start(bf16[1,2,4,144,128]{4,3,2,1,0:T(8,128)(2,1)S(1)} %get-tuple-element.31), channel_id=1, source_target_pairs={{8,0},{16,8},{24,16},{0,24},{9,1},{17,9},{25,17},{1,25},{10,2},{18... | collective-permute-start | bytes 884744 | tf_op jit(solution)/shard_map/ppermute | solution.py:72
  21.8 11.8 %collective-permute-start.3 = (bf16[4,2,1,144,128]{4,3,2,1,0:T(8,128)(2,1)S(1)}, bf16[4,2,1,144,128]{4,3,2,1,0:T(8,128)(2,1)S(1)}, u32[]{:S(2)}, u32[]{:S(2)}) collective-permute-start(bf16[4,2,1,144,128]{4,3,2,1,0:T(8,128)(2,1)S(1)} %get-tuple-element.26), channel_id=1, source_target_pairs={{0,1},{1,2},{2,3},{3,0},{4,5},{5,6},{6,7},{7,4},{8,9},{9,10},{10,1... | collective-permute-start | bytes 884744 | tf_op jit(solution)/shard_map/ppermute | solution.py:71
  23.4 15.7 %collective-permute-start.4 = (bf16[4,2,1,144,128]{4,3,2,1,0:T(8,128)(2,1)S(1)}, bf16[4,2,1,144,128]{4,3,2,1,0:T(8,128)(2,1)S(1)}, u32[]{:S(2)}, u32[]{:S(2)}) collective-permute-start(bf16[4,2,1,144,128]{4,3,2,1,0:T(8,128)(2,1)S(1)} %get-tuple-element.27), channel_id=1, source_target_pairs={{1,0},{2,1},{3,2},{0,3},{5,4},{6,5},{7,6},{4,7},{9,8},{10,9},{11,1... | collective-permute-start | bytes 884744 | tf_op jit(solution)/shard_map/ppermute | solution.py:72
  39.3 0.7 copy-start.5
  39.3 0.7 copy-start.4
  39.4 1.0 copy-start
  39.4 1.0 copy-start.1
  52.4 15.3 %all-to-all-start = ((bf16[32,32,128]{2,1,0:T(8,128)(2,1)}), bf16[32,32,128]{2,1,0:T(8,128)(2,1)S(1)}, u32[]{:S(2)}, u32[]{:S(2)}) async-start(bf16[32,32,128]{2,1,0:T(8,128)(2,1)} %bitcast.13), calls=%async_computation | async-start | bytes 524288 | tf_op jit(solution)/shard_map/all_to_all | solution.py:248
  71.0 15.8 %all-to-all-start.1 = ((bf16[32,48,128]{2,1,0:T(8,128)(2,1)}), bf16[32,48,128]{2,1,0:T(8,128)(2,1)S(1)}, u32[]{:S(2)}, u32[]{:S(2)}) async-start(bf16[32,48,128]{2,1,0:T(8,128)(2,1)} %bitcast.15), calls=%async_computation.1 | async-start | bytes 786432 | tf_op jit(solution)/shard_map/all_to_all | solution.py:248
  92.4 21.1 %copy-start.3 = (f32[1,1024]{1,0:T(1,128)}, f32[1,1024]{1,0:T(1,128)S(1)}, u32[]{:S(2)}) copy-start(f32[1,1024]{1,0:T(1,128)S(1)} %slice.46) | copy-start | bytes 12292
  92.7 8.5 %collective-permute-start.5 = (bf16[2,1,4,128,128]{4,3,2,1,0:T(8,128)(2,1)S(1)}, bf16[2,1,4,128,128]{4,3,2,1,0:T(8,128)(2,1)S(1)}, u32[]{:S(2)}, u32[]{:S(2)}) collective-permute-start(bf16[2,1,4,128,128]{4,3,2,1,0:T(8,128)(2,1)S(1)} %multiply_convert_fusion.1), channel_id=1, source_target_pairs={{0,4},{4,0},{1,5},{5,1},{2,6},{6,2},{3,7},{7,3},{8,12},{12,8},{9,1... | collective-permute-start | bytes 786440 | tf_op jit(solution)/shard_map/ppermute | solution.py:68
  101.2 7.8 %collective-permute-start.6 = (bf16[1,2,4,128,128]{4,3,2,1,0:T(8,128)(2,1)S(1)}, bf16[1,2,4,128,128]{4,3,2,1,0:T(8,128)(2,1)S(1)}, u32[]{:S(2)}, u32[]{:S(2)}) collective-permute-start(bf16[1,2,4,128,128]{4,3,2,1,0:T(8,128)(2,1)S(1)} %get-tuple-element.32), channel_id=1, source_target_pairs={{0,8},{8,16},{16,24},{24,0},{1,9},{9,17},{17,25},{25,1},{2,10},{10... | collective-permute-start | bytes 786440 | tf_op jit(solution)/shard_map/ppermute | solution.py:71
  101.3 7.8 %collective-permute-start.7 = (bf16[1,2,4,128,128]{4,3,2,1,0:T(8,128)(2,1)S(1)}, bf16[1,2,4,128,128]{4,3,2,1,0:T(8,128)(2,1)S(1)}, u32[]{:S(2)}, u32[]{:S(2)}) collective-permute-start(bf16[1,2,4,128,128]{4,3,2,1,0:T(8,128)(2,1)S(1)} %get-tuple-element.33), channel_id=1, source_target_pairs={{8,0},{16,8},{24,16},{0,24},{9,1},{17,9},{25,17},{1,25},{10,2},{18... | collective-permute-start | bytes 786440 | tf_op jit(solution)/shard_map/ppermute | solution.py:72
  109.1 11.1 %collective-permute-start.8 = (bf16[4,2,1,128,128]{4,3,2,1,0:T(8,128)(2,1)S(1)}, bf16[4,2,1,128,128]{4,3,2,1,0:T(8,128)(2,1)S(1)}, u32[]{:S(2)}, u32[]{:S(2)}) collective-permute-start(bf16[4,2,1,128,128]{4,3,2,1,0:T(8,128)(2,1)S(1)} %get-tuple-element.28), channel_id=1, source_target_pairs={{0,1},{1,2},{2,3},{3,0},{4,5},{5,6},{6,7},{7,4},{8,9},{9,10},{10,1... | collective-permute-start | bytes 786440 | tf_op jit(solution)/shard_map/ppermute | solution.py:71
  109.2 14.5 %collective-permute-start.9 = (bf16[4,2,1,128,128]{4,3,2,1,0:T(8,128)(2,1)S(1)}, bf16[4,2,1,128,128]{4,3,2,1,0:T(8,128)(2,1)S(1)}, u32[]{:S(2)}, u32[]{:S(2)}) collective-permute-start(bf16[4,2,1,128,128]{4,3,2,1,0:T(8,128)(2,1)S(1)} %get-tuple-element.29), channel_id=1, source_target_pairs={{1,0},{2,1},{3,2},{0,3},{5,4},{6,5},{7,6},{4,7},{9,8},{10,9},{11,1... | collective-permute-start | bytes 786440 | tf_op jit(solution)/shard_map/ppermute | solution.py:72
  113.7 10.2 %copy-start.2 = (bf16[128,128]{1,0:T(8,128)(2,1)S(1)}, bf16[128,128]{1,0:T(8,128)(2,1)}, u32[]{:S(2)}) copy-start(bf16[128,128]{1,0:T(8,128)(2,1)} %msg_ref.1) | copy-start | bytes 98308

commit v2 on v1

--- a/solution.py
+++ b/solution.py
@@ -60,23 +60,207 @@
     return 1 + offset
 
 
-def with_halo(shard, axis, dim):
-    devices, length = lax.axis_size(axis), shard.shape[dim]
-    up = [(i, (i + 1) % devices) for i in range(devices)]
-    down = [(j, i) for i, j in up]
-    if devices == 2 and length == 1:
-        return jnp.concatenate([shard, lax.ppermute(shard, axis, up)], axis=dim)
-    last = lax.slice_in_dim(shard, length - 1, length, axis=dim)
-    first = lax.slice_in_dim(shard, 0, 1, axis=dim)
-    before = lax.ppermute(last, axis, up)
-    after = lax.ppermute(first, axis, down)
-    return jnp.concatenate([before, shard, after], axis=dim)
-
-
-def exchange_halo(shard):
-    shard = with_halo(shard, "gy", 1)
-    shard = with_halo(shard, "gx", 0)
-    return with_halo(shard, "gz", 2)
+def coordinates(index, counts):
+    return (index // (counts[1] * counts[2]), index // counts[2] % counts[1], index % counts[2])
+
+
+def halo_plan(counts, lengths):
+    doubled = [n == 2 and length == 1 for n, length in zip(counts, lengths)]
+    own = [(0, 1) if two else (1, 1 + length) for two, length in zip(doubled, lengths)]
+
+    def faces(d):
+        if doubled[d]:
+            return {1: ((0, 1), (1, 2))}
+        length = lengths[d]
+        return {1: ((length, length + 1), (0, 1)), -1: ((1, 2), (length + 1, length + 2))}
+
+    moves = []
+
+    def add(d, way, source, target, need):
+        moves.append((d, way, tuple(source), tuple(target), need))
+        return len(moves) - 1
+
+    lines = [(own[1], None)]
+    for way, (source, target) in faces(1).items():
+        lines.append(
+            (target, add(1, way, (own[0], source, own[2]), (own[0], target, own[2]), None))
+        )
+    sheets = []
+    for at_y, need_y in lines:
+        sheets.append((own[0], at_y, need_y))
+        for way, (source, target) in faces(0).items():
+            need = add(0, way, (source, at_y, own[2]), (target, at_y, own[2]), need_y)
+            sheets.append((target, at_y, need))
+    for at_x, at_y, need in sheets:
+        for way, (source, target) in faces(2).items():
+            add(2, way, (at_x, at_y, source), (at_x, at_y, target), need)
+    padded = tuple(length + (1 if two else 2) for two, length in zip(doubled, lengths))
+    return padded, own, moves
+
+
+def halo_kernel(counts, lengths, src_ref, out_ref, send_sem, recv_sem, own_sem):
+    padded, own, moves = halo_plan(counts, lengths)
+    me = [lax.axis_index(a) for a in AXES]
+
+    def neighbour(d, way):
+        where = list(me)
+        where[d] = lax.rem(me[d] + way + counts[d], counts[d])
+        return tuple(where)
+
+    barrier = pltpu.get_barrier_semaphore()
+    links = sorted({(d, way) for d, way, *_ in moves})
+    for d, way in links:
+        pl.semaphore_signal(
+            barrier, inc=1, device_id=neighbour(d, way), device_id_type=pl.DeviceIdType.MESH
+        )
+    pl.semaphore_wait(barrier, len(links))
+
+    def region(ref, spans, shift=(0, 0, 0)):
+        return ref.at[tuple(slice(lo - s, hi - s) for (lo, hi), s in zip(spans, shift))]
+
+    starts = [lo for lo, _ in own]
+    copies = []
+    for which, (d, way, source, target, need) in enumerate(moves):
+        origin = region(src_ref, source, starts) if need is None else region(out_ref, source)
+        copies.append(
+            pltpu.make_async_remote_copy(
+                src_ref=origin,
+                dst_ref=region(out_ref, target),
+                send_sem=send_sem.at[which],
+                recv_sem=recv_sem.at[which],
+                device_id=neighbour(d, way),
+                device_id_type=pl.DeviceIdType.MESH,
+            )
+        )
+    keep = pltpu.make_async_copy(src_ref, region(out_ref, own), own_sem)
+    ready = [w for w, m in enumerate(moves) if m[4] is None]
+    for which in ready:
+        copies[which].start()
+    keep.start()
+    waited = set()
+
+    def forward(which):
+        copies[which].wait_recv()
+        waited.add(which)
+        for later, move in enumerate(moves):
+            if move[4] == which:
+                copies[later].start()
+
+    direct = [w for w in ready if moves[w][0] == 0]
+    for which in direct:
+        forward(which)
+    for which in [w for w in ready if moves[w][0] == 1]:
+        forward(which)
+    for which, move in enumerate(moves):
+        if which not in waited and any(m[4] == which for m in moves):
+            forward(which)
+    for which in range(len(moves)):
+        if which not in waited:
+            copies[which].wait_recv()
+    for copy in copies:
+        copy.wait_send()
+    keep.wait()
+
+
+def exchange_halo(shard, number, counts):
+    lengths = shard.shape[:3]
+    padded, _, moves = halo_plan(counts, lengths)
+    return pl.pallas_call(
+        functools.partial(halo_kernel, counts, lengths),
+        out_shape=jax.ShapeDtypeStruct(padded + shard.shape[3:], shard.dtype),
+        in_specs=[pl.BlockSpec(memory_space=pltpu.VMEM)],
+        out_specs=pl.BlockSpec(memory_space=pl.ANY),
+        scratch_shapes=[
+            pltpu.SemaphoreType.DMA((len(moves),)),
+            pltpu.SemaphoreType.DMA((len(moves),)),
+            pltpu.SemaphoreType.DMA,
+        ],
+        compiler_params=params(collective_id=number, has_side_effects=True),
+        name="halo",
+    )(shard)
+
+
+def swap_kernel(counts, senders, receivers, src_ref, out_ref, send_sem, recv_sem, own_sem):
+    total = counts[0] * counts[1] * counts[2]
+    chunks = src_ref.shape[0]
+    me = (lax.axis_index("gx") * counts[1] + lax.axis_index("gy")) * counts[2] + lax.axis_index("gz")
+    barrier = pltpu.get_barrier_semaphore()
+
+    def chunk(q):
+        return lax.rem(q, chunks)
+
+    def greet(k, carry):
+        pl.semaphore_signal(
+            barrier,
+            inc=1,
+            device_id=coordinates(lax.rem(me + k, total), counts),
+            device_id_type=pl.DeviceIdType.MESH,
+        )
+        return carry
+
+    lax.fori_loop(1, total, greet, 0)
+    keep = pltpu.make_async_copy(src_ref.at[chunk(me)], out_ref.at[me], own_sem)
+    keep.start()
+    pl.semaphore_wait(barrier, total - 1)
+
+    def copy(k):
+        to = lax.rem(me + k, total)
+        return to, pltpu.make_async_remote_copy(
+            src_ref=src_ref.at[chunk(to)],
+            dst_ref=out_ref.at[me],
+            send_sem=send_sem.at[k],
+            recv_sem=recv_sem.at[k],
+            device_id=coordinates(to, counts),
+            device_id_type=pl.DeviceIdType.MESH,
+        )
+
+    def guarded(fact, act):
+        if fact is None:
+            act()
+        else:
+            pl.when(fact)(act)
+
+    def sends(to):
+        if senders < total:
+            return me < senders
+        return None if receivers == total else to < receivers
+
+    def takes(source):
+        if receivers < total:
+            return me < receivers
+        return None if senders == total else source < senders
+
+    def begin(k, carry):
+        to, move = copy(k)
+        guarded(sends(to), lambda: move.start())
+        return carry
+
+    def finish(k, carry):
+        to, move = copy(k)
+        guarded(takes(lax.rem(me - k + total, total)), lambda: move.wait_recv())
+        guarded(sends(to), lambda: move.wait_send())
+        return carry
+
+    lax.fori_loop(1, total, begin, 0)
+    lax.fori_loop(1, total, finish, 0)
+    keep.wait()
+
+
+def exchange_planes(payload, number, counts, senders, receivers):
+    total = counts[0] * counts[1] * counts[2]
+    return pl.pallas_call(
+        functools.partial(swap_kernel, counts, senders, receivers),
+        out_shape=jax.ShapeDtypeStruct((total,) + payload.shape[1:], payload.dtype),
+        in_specs=[pl.BlockSpec(memory_space=pltpu.VMEM)],
+        out_specs=pl.BlockSpec(memory_space=pl.ANY),
+        scratch_shapes=[
+            pltpu.SemaphoreType.DMA((total,)),
+            pltpu.SemaphoreType.DMA((total,)),
+            pltpu.SemaphoreType.DMA,
+        ],
+        compiler_params=params(collective_id=number, has_side_effects=True),
+        name="swap",
+    )(payload)
 
 
 def pair_total(cells, counts, centre, table_ref, near_ref, value_ref):
@@ -244,10 +428,6 @@
     return jnp.where(squared > 0, jnp.exp(-((math.pi * spread_width) ** 2) * squared) / safe, 0.0)
 
 
-def exchange_planes(payload):
-    return lax.all_to_all(payload, AXES, split_axis=0, concat_axis=0, tiled=True)
-
-
 def params(**kw):
     return pltpu.CompilerParams(vmem_limit_bytes=48 * 1024 * 1024, **kw)
 
@@ -283,7 +463,7 @@
     ).astype(bf16).reshape(number, 16, slots)
     table = offset_table()
 
-    padded = exchange_halo(jnp.concatenate([projected, near], axis=3))
+    padded = exchange_halo(jnp.concatenate([projected, near], axis=3), 0, counts)
     values = padded[:, :, :, :slots]
     nears = padded[:, :, :, slots:]
 
@@ -331,9 +511,7 @@
         compiler_params=params(),
         name="spread",
     )(corner, fraction, charges, wave_x).reshape(owners, rows, LANES)
-    if owners < devices:
-        payload = jnp.pad(payload, ((0, devices - owners), (0, 0), (0, 0)))
-    got = exchange_planes(payload)
+    got = exchange_planes(payload, 2, counts, devices, owners)
 
     range_y = jnp.arange(size[1], dtype=jnp.int32)
     range_z = jnp.arange(size[2], dtype=jnp.int32)
@@ -363,7 +541,7 @@
         compiler_params=params(),
         name="planes",
     )(got, wide_z, wide_y, influence)
-    field = exchange_planes(jnp.tile(solved, (counts[0], 1, 1)))
+    field = exchange_planes(solved, 3, counts, owners, devices)
 
     potential, energy = pl.pallas_call(
         functools.partial(
@@ -384,7 +562,7 @@
     sigma = jax.nn.sigmoid(pre)
     slope = sigma * (1.0 + pre * (1.0 - sigma))
     cotangent = (potential[..., None] * charge_weight.astype(f32) * slope).astype(bf16)
-    cots = exchange_halo(cotangent)
+    cots = exchange_halo(cotangent, 1, counts)
     grad = pl.pallas_call(
         functools.partial(back_kernel, cells, counts),
         out_shape=jax.ShapeDtypeStruct(square, f32),

time: 133 us -> 104 us (0.78)
  waiting for transfers between devices: 69.8 us -> 0 us
  Pallas kernels: 28.1 us -> 95.2 us
  starting transfers between devices: 22.5 us -> 0 us
  local copies, waits for them, and re-layouts: 4.47 us -> 3 us
  other arithmetic: 4.96 us -> 3.62 us
    pallas_call x0 -> x4, Pallas kernels: none -> 67.8 us  [the longest x2 40.8 us: exchange_halo(): pl.pallas_call(functools.partial(halo_kernel, counts, lengths), out_shape...]
    ppermute x10 -> x0, waiting for transfers between devices: 46.6 us -> none  [the longest x4 24.6 us: with_halo(): before = lax.ppermute(last, axis, up)]
    all_to_all x2 -> x0, waiting for transfers between devices: 23.2 us -> none  [exchange_planes(): lax.all_to_all(payload, AXES, split_axis=0, concat_axis=0, tiled=True)]
    ppermute x10 -> x0, starting transfers between devices: 15.3 us -> none  [the longest x4 9.53 us: with_halo(): after = lax.ppermute(first, axis, down)]
    all_to_all x2 -> x0, starting transfers between devices: 7.15 us -> none  [exchange_planes(): lax.all_to_all(payload, AXES, split_axis=0, concat_axis=0, tiled=True)]
  transfers between devices with their start and end apart: 12 -> 0, of which waited for: 11 -> 0; matrix products, arithmetic and copies ran while one was open for 4% -> 0% of each run, Pallas kernels for 0% -> 0%
where the time goes in v2:
time: 104 us
  Pallas kernels  95.2 us (92%)
  other arithmetic  3.62 us (3%)
  local copies, waits for them, and re-layouts  3 us (3%)
  matrix products  1.16 us (1%)
    pallas_call x2, Pallas kernels, exchange_halo(): pl.pallas_call(functools.partial(halo_kernel, counts, lengths), out_shape...  40.8 us
    pallas_call x2, Pallas kernels, exchange_planes(): pl.pallas_call(functools.partial(swap_kernel, counts, senders, receivers)...  27 us
    pallas_call x1, Pallas kernels, body(): pl.pallas_call(functools.partial(message_kernel, cells, counts), out_shap...  8.21 us
    pallas_call x1, Pallas kernels, body(): pl.pallas_call(functools.partial(back_kernel, cells, counts), out_shape=j...  8 us
    pallas_call x1, Pallas kernels, body(): pl.pallas_call(functools.partial(field_kernel, (local[0], local[1], local...  5.6 us
    pallas_call x1, Pallas kernels, body(): pl.pallas_call(functools.partial(spread_kernel, (local[0], local[1], loca...  3.09 us
    pallas_call x1, Pallas kernels, body(): pl.pallas_call(functools.partial(plane_kernel, (counts[1], counts[2], pac...  2.45 us

profile of v2, /device:TPU:0, one launch (start us, length us, event | category | flops | bytes accessed | tf_op | source)
XLA Modules:
  0.0 103.9 jit_solution(4640653924496016209)
XLA Ops:
  0.6 0.8 fusion.32
  1.4 0.2 concatenate.51.centre_ref
  1.7 1.2 %convolution_convert_fusion = bf16[1024,128]{1,0:T(8,128)(2,1)S(1)} fusion(bf16[1024,128]{1,0:T(8,128)(2,1)} %bitcast.55, bf16[128,128]{1,0:T(8,128)(2,1)} %msg_ref.1), kind=kOutput, calls=%fused_computation | convolution fusion | flops 33685504 | bytes 557056 | tf_op jit(solution)/shard_map/dot_general | solution.py:452
  2.9 0.3 concatenate.57.src_ref
  3.2 22.7 %halo.2 = bf16[4,2,6,144,128]{4,3,2,1,0:T(8,128)(2,1)S(1)} custom-call(bf16[2,1,4,144,128]{4,3,2,1,0:T(8,128)(2,1)S(1)} %concatenate.57.src_ref), custom_call_target="tpu_custom_call" | custom-call | tf_op jit(solution)/shard_map/halo/pallas_call | solution.py:168
  25.9 0.2 slice.16.value_ref
  26.1 0.4 copy-done.7
  26.7 0.1 copy-done
  26.9 8.2 %message.1 = (f32[8,128,128]{2,1,0:T(8,128)S(1)}, f32[8,8,128]{2,1,0:T(8,128)S(1)}) custom-call(bf16[8,16,128]{2,1,0:T(8,128)(2,1)S(1)} %concatenate.51.centre_ref, bf16[27,16,128]{2,1,0:T(8,128)(2,1)S(1)} %broadcast_in_dim.8.table_ref, bf16[4,2,6,16,128]{4,3,2,1,0:T(8,128)(2,1)S(1)} %slice.15.near_ref, bf16[4,2,6,128,128]{4,3,2,1,0:T(8,128)(2,1)S(1)} %slice.16.value_ref, ...), custom_call_target="tpu_custom_call" | custom-call | tf_op jit(solution)/shard_map/message/pallas_call | solution.py:473
  35.3 0.1 add.236
  35.5 0.3 sine_add_fusion.1.wave_ref
  36.2 3.1 %spread.1 = bf16[1024,128]{1,0:T(8,128)(2,1)S(1)} custom-call(s32[3,1024]{1,0:T(4,128)S(1)} %reshape.564.corner_ref, f32[3,1024]{1,0:T(4,128)S(1)} %reshape.565.fraction_ref, f32[1,1024]{1,0:T(1,128)S(1)} %slice_bitcast_fusion.charge_ref, f32[128,32]{1,0:T(8,128)S(1)} %sine_add_fusion.1.wave_ref), custom_call_target="tpu_custom_call" | custom-call | tf_op jit(solution)/shard_map/spread/pallas_call | solution.py:504
  39.3 13.2 %swap.2.got_ref = bf16[32,32,128]{2,1,0:T(8,128)(2,1)S(1)} custom-call(bf16[32,32,128]{2,1,0:T(8,128)(2,1)S(1)} %bitcast.57), custom_call_target="tpu_custom_call" | custom-call | tf_op jit(solution)/shard_map/swap/pallas_call | solution.py:251
  52.9 1.1 %sine_add_fusion = f32[4,1,64,256]{3,2,1,0:T(8,128)S(1)} fusion(s32[4,64]{1,0:T(4,128)S(1)} %multiply_add_fusion), kind=kLoop, calls=%fused_computation.13 | loop fusion | flops 983040 | bytes 263168 | tf_op jit(solution)/shard_map/add | solution.py:41
  54.1 0.2 sine_add_fusion.2
  54.5 0.2 reshape.568
  54.9 2.4 %planes.1.src_ref = bf16[8,48,128]{2,1,0:T(8,128)(2,1)S(1)} custom-call(bf16[32,32,128]{2,1,0:T(8,128)(2,1)S(1)} %swap.2.got_ref, f32[4,2,128,256]{3,2,1,0:T(8,128)S(1)} %select_maximum_fusion.z_ref, f32[128,128]{1,0:T(8,128)S(1)} %copy.53.y_ref, f32[128,256]{1,0:T(8,128)S(1)} %fusion.6.g_ref), custom_call_target="tpu_custom_call" | custom-call | tf_op jit(solution)/shard_map/planes/pallas_call | solution.py:538
  57.3 13.8 %swap.3.got_ref = bf16[32,48,128]{2,1,0:T(8,128)(2,1)S(1)} custom-call(bf16[8,48,128]{2,1,0:T(8,128)(2,1)S(1)} %planes.1.src_ref), custom_call_target="tpu_custom_call" | custom-call | tf_op jit(solution)/shard_map/swap/pallas_call | solution.py:251
  71.1 5.6 %field.1 = (f32[8,1024]{1,0:T(8,128)S(1)}, f32[8,128]{1,0:T(8,128)S(1)}) custom-call(s32[3,1024]{1,0:T(4,128)S(1)} %reshape.564.corner_ref, f32[3,1024]{1,0:T(4,128)S(1)} %reshape.565.fraction_ref, f32[128,32]{1,0:T(8,128)S(1)} %sine_add_fusion.1.wave_ref, bf16[32,48,128]{2,1,0:T(8,128)(2,1)S(1)} %swap.3.got_ref), custom_call_target="tpu_custom_call" | custom-call | tf_op jit(solution)/shard_map/field/pallas_call | solution.py:546
  76.8 0.2 multiply_convert_fusion.cot_ref
  77.0 0.2 multiply_convert_fusion.1.src_ref
  77.2 18.2 %halo.3.value_ref = bf16[4,2,6,128,128]{4,3,2,1,0:T(8,128)(2,1)S(1)} custom-call(bf16[2,1,4,128,128]{4,3,2,1,0:T(8,128)(2,1)S(1)} %multiply_convert_fusion.1.src_ref), custom_call_target="tpu_custom_call" | custom-call | tf_op jit(solution)/shard_map/halo/pallas_call | solution.py:168
  95.4 8.0 %back.1 = f32[8,128,128]{2,1,0:T(8,128)} custom-call(bf16[8,16,128]{2,1,0:T(8,128)(2,1)S(1)} %concatenate.51.centre_ref, bf16[27,16,128]{2,1,0:T(8,128)(2,1)S(1)} %broadcast_in_dim.8.table_ref, bf16[4,2,6,16,128]{4,3,2,1,0:T(8,128)(2,1)S(1)} %slice.15.near_ref, bf16[4,2,6,128,128]{4,3,2,1,0:T(8,128)(2,1)S(1)} %halo.3.value_ref, ...), custom_call_target="tpu_custom_call" | custom-call | tf_op jit(solution)/shard_map/back/pallas_call | solution.py:566
  103.4 0.5 slice.19
  (60 shorter events, 1.7 us)
Async XLA Ops:
  25.9 0.7 copy-start.7
  25.9 0.7 copy-start.6
  25.9 1.0 copy-start
  25.9 1.0 copy-start.1
  26.5 9.5 %copy-start.3 = (s32[2,1,4,3,128]{4,2,3,1,0:T(4,128)S(1)}, s32[2,1,4,3,128]{4,2,3,1,0:T(4,128)}, u32[]{:S(2)}) copy-start(s32[2,1,4,3,128]{4,2,3,1,0:T(4,128)} %param.11) | copy-start | bytes 36868
  26.5 9.6 %copy-start.4 = (f32[2,1,4,3,128]{4,2,3,1,0:T(4,128)S(1)}, f32[2,1,4,3,128]{4,2,3,1,0:T(4,128)}, u32[]{:S(2)}) copy-start(f32[2,1,4,3,128]{4,2,3,1,0:T(4,128)} %param.12) | copy-start | bytes 36868
  76.7 18.7 %copy-start.5 = (f32[1,1024]{1,0:T(1,128)}, f32[1,1024]{1,0:T(1,128)S(1)}, u32[]{:S(2)}) copy-start(f32[1,1024]{1,0:T(1,128)S(1)} %slice.18) | copy-start | bytes 12292
  76.7 18.7 %copy-start.2 = (bf16[128,128]{1,0:T(8,128)(2,1)S(1)}, bf16[128,128]{1,0:T(8,128)(2,1)}, u32[]{:S(2)}) copy-start(bf16[128,128]{1,0:T(8,128)(2,1)} %msg_ref.1) | copy-start | bytes 98308

commit v3 on v2

--- a/solution.py
+++ b/solution.py
@@ -80,20 +80,20 @@
         moves.append((d, way, tuple(source), tuple(target), need))
         return len(moves) - 1
 
-    lines = [(own[1], None)]
-    for way, (source, target) in faces(1).items():
+    lines = [(own[2], None)]
+    for way, (source, target) in faces(2).items():
         lines.append(
-            (target, add(1, way, (own[0], source, own[2]), (own[0], target, own[2]), None))
+            (target, add(2, way, (own[0], own[1], source), (own[0], own[1], target), None))
         )
     sheets = []
-    for at_y, need_y in lines:
-        sheets.append((own[0], at_y, need_y))
+    for at_z, need_z in lines:
+        sheets.append((own[1], at_z, need_z))
+        for way, (source, target) in faces(1).items():
+            need = add(1, way, (own[0], source, at_z), (own[0], target, at_z), need_z)
+            sheets.append((target, at_z, need))
+    for at_y, at_z, need in sheets:
         for way, (source, target) in faces(0).items():
-            need = add(0, way, (source, at_y, own[2]), (target, at_y, own[2]), need_y)
-            sheets.append((target, at_y, need))
-    for at_x, at_y, need in sheets:
-        for way, (source, target) in faces(2).items():
-            add(2, way, (at_x, at_y, source), (at_x, at_y, target), need)
+            add(0, way, (source, at_y, at_z), (target, at_y, at_z), need)
     padded = tuple(length + (1 if two else 2) for two, length in zip(doubled, lengths))
     return padded, own, moves
 
@@ -146,11 +146,6 @@
             if move[4] == which:
                 copies[later].start()
 
-    direct = [w for w in ready if moves[w][0] == 0]
-    for which in direct:
-        forward(which)
-    for which in [w for w in ready if moves[w][0] == 1]:
-        forward(which)
     for which, move in enumerate(moves):
         if which not in waited and any(m[4] == which for m in moves):
             forward(which)
@@ -268,19 +263,24 @@
     at_z = index % cells[2]
     at_y = index // cells[2] % cells[1]
     at_x = index // (cells[2] * cells[1])
-    total = jnp.zeros((centre.shape[1], value_ref.shape[-1]), f32)
-    for which, o in enumerate(offsets()):
-        where = [
+    total = None
+
+    def cell_at(o):
+        return tuple(
             base + slot(step, count, length)
             for base, step, count, length in zip((at_x, at_y, at_z), o, counts, cells)
-        ]
-        near = near_ref[where[0], where[1], where[2]] * table_ref[which]
+        )
+
+    every = list(enumerate(offsets()))
+    for first in range(0, len(every), 2):
+        group = every[first : first + 2]
+        near = jnp.concatenate([near_ref[cell_at(o)] * table_ref[w] for w, o in group], axis=1)
+        values = jnp.concatenate([value_ref[cell_at(o)] for _, o in group], axis=0)
         inside = lax.dot_general(centre, near, TN, preferred_element_type=f32)
         inside = jnp.maximum(inside, 0.0)
         weight = (pair_scale * inside * inside).astype(bf16)
-        total = total + jnp.dot(
-            weight, value_ref[where[0], where[1], where[2]], preferred_element_type=f32
-        )
+        part = jnp.dot(weight, values, preferred_element_type=f32)
+        total = part if total is None else total + part
     return total
 
 

time: 104 us -> 99.4 us (0.956)
  Pallas kernels: 95.2 us -> 90.2 us
    pallas_call x2, Pallas kernels: 40.8 us -> 33.5 us  [exchange_halo(): pl.pallas_call(functools.partial(halo_kernel, counts, lengths), out_shape...]
    pallas_call x1, Pallas kernels: 8.21 us -> 10.1 us  [body(): pl.pallas_call(functools.partial(message_kernel, cells, counts), out_shap...]
where the time goes in v3:
time: 99.4 us; the launch traced here: 99 us
  Pallas kernels  90.2 us (91%)
  other arithmetic  3.58 us (4%)
  local copies, waits for them, and re-layouts  3 us (3%)
  matrix products  1.16 us (1%)
    pallas_call x2, Pallas kernels, exchange_halo(): pl.pallas_call(functools.partial(halo_kernel, counts, lengths), out_shape...  33.5 us
    pallas_call x2, Pallas kernels, exchange_planes(): pl.pallas_call(functools.partial(swap_kernel, counts, senders, receivers)...  27.6 us
    pallas_call x1, Pallas kernels, body(): pl.pallas_call(functools.partial(message_kernel, cells, counts), out_shap...  10.1 us
    pallas_call x1, Pallas kernels, body(): pl.pallas_call(functools.partial(back_kernel, cells, counts), out_shape=j...  7.86 us
    pallas_call x1, Pallas kernels, body(): pl.pallas_call(functools.partial(field_kernel, (local[0], local[1], local...  5.61 us
    pallas_call x1, Pallas kernels, body(): pl.pallas_call(functools.partial(spread_kernel, (local[0], local[1], loca...  3.09 us
    pallas_call x1, Pallas kernels, body(): pl.pallas_call(functools.partial(plane_kernel, (counts[1], counts[2], pac...  2.44 us

profile of v3, /device:TPU:0, one launch (start us, length us, event | category | flops | bytes accessed | tf_op | source)
XLA Modules:
  0.0 99.0 jit_solution(13525244843079761228)
XLA Ops:
  0.6 0.8 fusion.32
  1.4 0.2 concatenate.51.centre_ref
  1.7 1.2 %convolution_convert_fusion = bf16[1024,128]{1,0:T(8,128)(2,1)S(1)} fusion(bf16[1024,128]{1,0:T(8,128)(2,1)} %bitcast.55, bf16[128,128]{1,0:T(8,128)(2,1)} %msg_ref.1), kind=kOutput, calls=%fused_computation | convolution fusion | flops 33685504 | bytes 557056 | tf_op jit(solution)/shard_map/dot_general | solution.py:452
  2.9 0.3 concatenate.57.src_ref
  3.2 19.0 %halo.2 = bf16[4,2,6,144,128]{4,3,2,1,0:T(8,128)(2,1)S(1)} custom-call(bf16[2,1,4,144,128]{4,3,2,1,0:T(8,128)(2,1)S(1)} %concatenate.57.src_ref), custom_call_target="tpu_custom_call" | custom-call | tf_op jit(solution)/shard_map/halo/pallas_call | solution.py:163
  22.3 0.2 slice.16.value_ref
  22.5 0.4 copy-done.7
  23.0 0.1 copy-done
  23.2 10.1 %message.1 = (f32[8,128,128]{2,1,0:T(8,128)S(1)}, f32[8,8,128]{2,1,0:T(8,128)S(1)}) custom-call(bf16[8,16,128]{2,1,0:T(8,128)(2,1)S(1)} %concatenate.51.centre_ref, bf16[27,16,128]{2,1,0:T(8,128)(2,1)S(1)} %broadcast_in_dim.8.table_ref, bf16[4,2,6,16,128]{4,3,2,1,0:T(8,128)(2,1)S(1)} %slice.15.near_ref, bf16[4,2,6,128,128]{4,3,2,1,0:T(8,128)(2,1)S(1)} %slice.16.value_ref, ...), custom_call_target="tpu_custom_call" | custom-call | tf_op jit(solution)/shard_map/message/pallas_call | solution.py:473
  33.4 0.1 add.236
  33.6 0.3 sine_add_fusion.1.wave_ref
  34.3 3.1 %spread.1 = bf16[1024,128]{1,0:T(8,128)(2,1)S(1)} custom-call(s32[3,1024]{1,0:T(4,128)S(1)} %reshape.564.corner_ref, f32[3,1024]{1,0:T(4,128)S(1)} %reshape.565.fraction_ref, f32[1,1024]{1,0:T(1,128)S(1)} %slice_bitcast_fusion.charge_ref, f32[128,32]{1,0:T(8,128)S(1)} %sine_add_fusion.1.wave_ref), custom_call_target="tpu_custom_call" | custom-call | tf_op jit(solution)/shard_map/spread/pallas_call | solution.py:504
  37.4 12.5 %swap.2.got_ref = bf16[32,32,128]{2,1,0:T(8,128)(2,1)S(1)} custom-call(bf16[32,32,128]{2,1,0:T(8,128)(2,1)S(1)} %bitcast.57), custom_call_target="tpu_custom_call" | custom-call | tf_op jit(solution)/shard_map/swap/pallas_call | solution.py:246
  50.3 1.1 %sine_add_fusion = f32[4,1,64,256]{3,2,1,0:T(8,128)S(1)} fusion(s32[4,64]{1,0:T(4,128)S(1)} %multiply_add_fusion), kind=kLoop, calls=%fused_computation.13 | loop fusion | flops 983040 | bytes 263168 | tf_op jit(solution)/shard_map/add | solution.py:41
  51.5 0.2 sine_add_fusion.2
  51.9 0.2 reshape.568
  52.3 2.4 %planes.1.src_ref = bf16[8,48,128]{2,1,0:T(8,128)(2,1)S(1)} custom-call(bf16[32,32,128]{2,1,0:T(8,128)(2,1)S(1)} %swap.2.got_ref, f32[4,2,128,256]{3,2,1,0:T(8,128)S(1)} %select_maximum_fusion.z_ref, f32[128,128]{1,0:T(8,128)S(1)} %copy.53.y_ref, f32[128,256]{1,0:T(8,128)S(1)} %fusion.6.g_ref), custom_call_target="tpu_custom_call" | custom-call | tf_op jit(solution)/shard_map/planes/pallas_call | solution.py:538
  54.7 15.2 %swap.3.got_ref = bf16[32,48,128]{2,1,0:T(8,128)(2,1)S(1)} custom-call(bf16[8,48,128]{2,1,0:T(8,128)(2,1)S(1)} %planes.1.src_ref), custom_call_target="tpu_custom_call" | custom-call | tf_op jit(solution)/shard_map/swap/pallas_call | solution.py:246
  69.9 5.6 %field.1 = (f32[8,1024]{1,0:T(8,128)S(1)}, f32[8,128]{1,0:T(8,128)S(1)}) custom-call(s32[3,1024]{1,0:T(4,128)S(1)} %reshape.564.corner_ref, f32[3,1024]{1,0:T(4,128)S(1)} %reshape.565.fraction_ref, f32[128,32]{1,0:T(8,128)S(1)} %sine_add_fusion.1.wave_ref, bf16[32,48,128]{2,1,0:T(8,128)(2,1)S(1)} %swap.3.got_ref), custom_call_target="tpu_custom_call" | custom-call | tf_op jit(solution)/shard_map/field/pallas_call | solution.py:546
  75.5 0.2 multiply_convert_fusion.cot_ref
  75.8 0.2 multiply_convert_fusion.1.src_ref
  76.0 14.5 %halo.3.value_ref = bf16[4,2,6,128,128]{4,3,2,1,0:T(8,128)(2,1)S(1)} custom-call(bf16[2,1,4,128,128]{4,3,2,1,0:T(8,128)(2,1)S(1)} %multiply_convert_fusion.1.src_ref), custom_call_target="tpu_custom_call" | custom-call | tf_op jit(solution)/shard_map/halo/pallas_call | solution.py:163
  90.6 7.9 %back.1 = f32[8,128,128]{2,1,0:T(8,128)} custom-call(bf16[8,16,128]{2,1,0:T(8,128)(2,1)S(1)} %concatenate.51.centre_ref, bf16[27,16,128]{2,1,0:T(8,128)(2,1)S(1)} %broadcast_in_dim.8.table_ref, bf16[4,2,6,16,128]{4,3,2,1,0:T(8,128)(2,1)S(1)} %slice.15.near_ref, bf16[4,2,6,128,128]{4,3,2,1,0:T(8,128)(2,1)S(1)} %halo.3.value_ref, ...), custom_call_target="tpu_custom_call" | custom-call | tf_op jit(solution)/shard_map/back/pallas_call | solution.py:566
  98.5 0.5 slice.19
  (60 shorter events, 1.6 us)
Async XLA Ops:
  22.2 0.7 copy-start.7
  22.2 0.7 copy-start.6
  22.2 1.0 copy-start
  22.2 1.0 copy-start.1
  22.9 11.3 %copy-start.3 = (s32[2,1,4,3,128]{4,2,3,1,0:T(4,128)S(1)}, s32[2,1,4,3,128]{4,2,3,1,0:T(4,128)}, u32[]{:S(2)}) copy-start(s32[2,1,4,3,128]{4,2,3,1,0:T(4,128)} %param.11) | copy-start | bytes 36868
  22.9 11.4 %copy-start.4 = (f32[2,1,4,3,128]{4,2,3,1,0:T(4,128)S(1)}, f32[2,1,4,3,128]{4,2,3,1,0:T(4,128)}, u32[]{:S(2)}) copy-start(f32[2,1,4,3,128]{4,2,3,1,0:T(4,128)} %param.12) | copy-start | bytes 36868
  75.5 15.1 %copy-start.5 = (f32[1,1024]{1,0:T(1,128)}, f32[1,1024]{1,0:T(1,128)S(1)}, u32[]{:S(2)}) copy-start(f32[1,1024]{1,0:T(1,128)S(1)} %slice.18) | copy-start | bytes 12292
  75.5 15.0 %copy-start.2 = (bf16[128,128]{1,0:T(8,128)(2,1)S(1)}, bf16[128,128]{1,0:T(8,128)(2,1)}, u32[]{:S(2)}) copy-start(bf16[128,128]{1,0:T(8,128)(2,1)} %msg_ref.1) | copy-start | bytes 98308

commit v4 on v3

--- a/solution.py
+++ b/solution.py
@@ -175,89 +175,6 @@
     )(shard)
 
 
-def swap_kernel(counts, senders, receivers, src_ref, out_ref, send_sem, recv_sem, own_sem):
-    total = counts[0] * counts[1] * counts[2]
-    chunks = src_ref.shape[0]
-    me = (lax.axis_index("gx") * counts[1] + lax.axis_index("gy")) * counts[2] + lax.axis_index("gz")
-    barrier = pltpu.get_barrier_semaphore()
-
-    def chunk(q):
-        return lax.rem(q, chunks)
-
-    def greet(k, carry):
-        pl.semaphore_signal(
-            barrier,
-            inc=1,
-            device_id=coordinates(lax.rem(me + k, total), counts),
-            device_id_type=pl.DeviceIdType.MESH,
-        )
-        return carry
-
-    lax.fori_loop(1, total, greet, 0)
-    keep = pltpu.make_async_copy(src_ref.at[chunk(me)], out_ref.at[me], own_sem)
-    keep.start()
-    pl.semaphore_wait(barrier, total - 1)
-
-    def copy(k):
-        to = lax.rem(me + k, total)
-        return to, pltpu.make_async_remote_copy(
-            src_ref=src_ref.at[chunk(to)],
-            dst_ref=out_ref.at[me],
-            send_sem=send_sem.at[k],
-            recv_sem=recv_sem.at[k],
-            device_id=coordinates(to, counts),
-            device_id_type=pl.DeviceIdType.MESH,
-        )
-
-    def guarded(fact, act):
-        if fact is None:
-            act()
-        else:
-            pl.when(fact)(act)
-
-    def sends(to):
-        if senders < total:
-            return me < senders
-        return None if receivers == total else to < receivers
-
-    def takes(source):
-        if receivers < total:
-            return me < receivers
-        return None if senders == total else source < senders
-
-    def begin(k, carry):
-        to, move = copy(k)
-        guarded(sends(to), lambda: move.start())
-        return carry
-
-    def finish(k, carry):
-        to, move = copy(k)
-        guarded(takes(lax.rem(me - k + total, total)), lambda: move.wait_recv())
-        guarded(sends(to), lambda: move.wait_send())
-        return carry
-
-    lax.fori_loop(1, total, begin, 0)
-    lax.fori_loop(1, total, finish, 0)
-    keep.wait()
-
-
-def exchange_planes(payload, number, counts, senders, receivers):
-    total = counts[0] * counts[1] * counts[2]
-    return pl.pallas_call(
-        functools.partial(swap_kernel, counts, senders, receivers),
-        out_shape=jax.ShapeDtypeStruct((total,) + payload.shape[1:], payload.dtype),
-        in_specs=[pl.BlockSpec(memory_space=pltpu.VMEM)],
-        out_specs=pl.BlockSpec(memory_space=pl.ANY),
-        scratch_shapes=[
-            pltpu.SemaphoreType.DMA((total,)),
-            pltpu.SemaphoreType.DMA((total,)),
-            pltpu.SemaphoreType.DMA,
-        ],
-        compiler_params=params(collective_id=number, has_side_effects=True),
-        name="swap",
-    )(payload)
-
-
 def pair_total(cells, counts, centre, table_ref, near_ref, value_ref):
     index = pl.program_id(0)
     at_z = index % cells[2]
@@ -271,15 +188,12 @@
             for base, step, count, length in zip((at_x, at_y, at_z), o, counts, cells)
         )
 
-    every = list(enumerate(offsets()))
-    for first in range(0, len(every), 2):
-        group = every[first : first + 2]
-        near = jnp.concatenate([near_ref[cell_at(o)] * table_ref[w] for w, o in group], axis=1)
-        values = jnp.concatenate([value_ref[cell_at(o)] for _, o in group], axis=0)
+    for which, o in enumerate(offsets()):
+        near = near_ref[cell_at(o)] * table_ref[which]
         inside = lax.dot_general(centre, near, TN, preferred_element_type=f32)
         inside = jnp.maximum(inside, 0.0)
         weight = (pair_scale * inside * inside).astype(bf16)
-        part = jnp.dot(weight, values, preferred_element_type=f32)
+        part = jnp.dot(weight, value_ref[cell_at(o)], preferred_element_type=f32)
         total = part if total is None else total + part
     return total
 
@@ -322,32 +236,8 @@
     )
 
 
-def spread_kernel(dims, corner_ref, fraction_ref, charge_ref, wave_ref, out_ref, hx_ref, left_ref):
-    local_x, local_y, local_z, pack = dims
-    rows_x = spline(corner_ref[0:1, :], fraction_ref[0:1, :], local_x)
-    rows_y = spline(corner_ref[1:2, :], fraction_ref[1:2, :], local_y)
-    hx_ref[...] = charge_ref[...] * jnp.dot(
-        wave_ref[...], rows_x, precision=highest, preferred_element_type=f32
-    )
-    half = hx_ref.shape[0] // pack
-    total = None
-    for h in range(pack):
-
-        def fill(k, carry):
-            left_ref[pl.ds(pl.multiple_of(k * local_y, local_y), local_y), :] = (
-                hx_ref[pl.ds(h * half + k, 1), :] * rows_y
-            ).astype(bf16)
-            return carry
-
-        lax.fori_loop(0, half, fill, 0, unroll=8)
-        right = spline(corner_ref[2:3, :], fraction_ref[2:3, :], LANES, h * local_z).astype(bf16)
-        part = lax.dot_general(left_ref[...], right, NT, preferred_element_type=f32)
-        total = part if total is None else total + part
-    out_ref[...] = total.astype(bf16)
-
-
-def plane_kernel(dims, count_x, got_ref, z_ref, y_ref, g_ref, out_ref):
-    count_y, count_z, pack = dims
+def solve_planes(counts, pack, got_ref, z_ref, y_ref, g_ref, out_ref):
+    count_x, count_y, count_z = counts
     rows = got_ref.shape[1]
     each = count_y * count_z
     halves = [None] * pack
@@ -385,34 +275,151 @@
             out_ref[b * count_z + c, rows : rows + 16, :] = tail.astype(bf16)
 
 
-def field_kernel(dims, scale, escale, owners, corner_ref, fraction_ref, wave_ref, got_ref, out_ref, energy_ref, hx_ref):
-    local_x, local_y, local_z, pack, rows = dims
+def mesh_kernel(
+    counts, local, pack, owners, scale, escale,
+    corner_ref, fraction_ref, charge_ref, wave_ref, z_ref, y_ref, g_ref,
+    out_ref, energy_ref,
+    hx_ref, left_ref, right_ref, payload_ref, got_ref, solved_ref, field_ref,
+    send_one, recv_one, send_two, recv_two,
+):
+    local_x, local_y, local_z = local
+    total = counts[0] * counts[1] * counts[2]
+    each = counts[1] * counts[2]
+    rows = payload_ref.shape[1]
+    per = rows // local_y
     atoms = corner_ref.shape[-1]
+    me = (lax.axis_index("gx") * counts[1] + lax.axis_index("gy")) * counts[2] + lax.axis_index("gz")
+    barrier = pltpu.get_barrier_semaphore()
+
+    def greet(k, carry):
+        pl.semaphore_signal(
+            barrier,
+            inc=1,
+            device_id=coordinates(lax.rem(me + k, total), counts),
+            device_id_type=pl.DeviceIdType.MESH,
+        )
+        return carry
+
+    lax.fori_loop(1, total, greet, 0)
+
     rows_x = spline(corner_ref[0:1, :], fraction_ref[0:1, :], local_x)
     rows_y = spline(corner_ref[1:2, :], fraction_ref[1:2, :], local_y)
+    charged = rows_y * charge_ref[...]
     hx_ref[...] = jnp.dot(wave_ref[...], rows_x, precision=highest, preferred_element_type=f32)
     half = hx_ref.shape[0] // pack
-    per = rows // local_y
-    acc = jnp.zeros((local_y, atoms), f32)
+    spread = None
     for h in range(pack):
+
+        def fill(k, carry):
+            left_ref[pl.ds(pl.multiple_of(k * local_y, local_y), local_y), :] = (
+                hx_ref[pl.ds(h * half + k, 1), :] * charged
+            ).astype(bf16)
+            return carry
+
+        lax.fori_loop(0, half, fill, 0, unroll=8)
         right = spline(corner_ref[2:3, :], fraction_ref[2:3, :], LANES, h * local_z).astype(bf16)
-
-        def step(q, acc):
-            block = got_ref[q, 0:rows, :]
-            value = jnp.dot(block, right, preferred_element_type=f32)
-            for k in range(per):
-                acc = acc + value[k * local_y : (k + 1) * local_y] * hx_ref[
-                    pl.ds(h * half + q * per + k, 1), :
-                ]
-            return acc
-
-        acc = lax.fori_loop(0, owners, step, acc, unroll=4)
+        right_ref[h] = right
+        part = lax.dot_general(left_ref[...], right, NT, preferred_element_type=f32)
+        spread = part if spread is None else spread + part
+    payload_ref[...] = spread.astype(bf16).reshape(payload_ref.shape)
+    got_ref[me] = payload_ref[jnp.minimum(me, owners - 1)]
+    pl.semaphore_wait(barrier, total - 1)
+
+    def guarded(fact, act):
+        if owners == total:
+            act()
+        else:
+            pl.when(fact)(act)
+
+    def copy(k, source, target, send, recv):
+        return pltpu.make_async_remote_copy(
+            src_ref=source,
+            dst_ref=target.at[me],
+            send_sem=send.at[k],
+            recv_sem=recv.at[k],
+            device_id=coordinates(lax.rem(me + k, total), counts),
+            device_id_type=pl.DeviceIdType.MESH,
+        )
+
+    def first(k):
+        to = lax.rem(me + k, total)
+        return to, copy(k, payload_ref.at[jnp.minimum(to, owners - 1)], got_ref, send_one, recv_one)
+
+    def second(k):
+        to = lax.rem(me + k, total)
+        return to, copy(k, solved_ref.at[lax.rem(to, each)], field_ref, send_two, recv_two)
+
+    def begin_one(k, carry):
+        to, move = first(k)
+        guarded(to < owners, lambda: move.start())
+        return carry
+
+    def arrive_one(k, carry):
+        to, move = first(k)
+        guarded(me < owners, lambda: move.wait_recv())
+        return carry
+
+    lax.fori_loop(1, total, begin_one, 0)
+    lax.fori_loop(1, total, arrive_one, 0)
+    solve_planes(counts, pack, got_ref, z_ref, y_ref, g_ref, solved_ref)
+
+    def begin_two(k, carry):
+        to, move = second(k)
+        guarded(me < owners, lambda: move.start())
+        return carry
+
+    lax.fori_loop(1, total, begin_two, 0)
+    field_ref[me] = solved_ref[lax.rem(me, each)]
+
+    group = 4 if total % 4 == 0 else 1
+
+    def gather(index, carry):
+        acc, tail = carry
+        sources, blocks = [], []
+        for i in range(group):
+            k = index * group + i
+            source = lax.rem(me - k + total, total)
+
+            def arrive(k=k):
+                second(k)[1].wait_recv()
+
+            if owners == total:
+                pl.when(k > 0)(arrive)
+            else:
+                pl.when((k > 0) & (source < owners))(arrive)
+            block = field_ref[source]
+            if owners < total:
+                block = jnp.where(source < owners, block.astype(f32), 0.0).astype(bf16)
+            sources.append(jnp.minimum(source, owners - 1))
+            blocks.append(block[0:rows])
+            tail = tail + block[rows:].astype(f32)
+        stack = jnp.concatenate(blocks, axis=0)
+        for h in range(pack):
+            value = jnp.dot(stack, right_ref[h], preferred_element_type=f32)
+            for i, source in enumerate(sources):
+                for k in range(per):
+                    at = (i * per + k) * local_y
+                    acc = acc + value[at : at + local_y] * hx_ref[
+                        pl.ds(h * half + source * per + k, 1), :
+                    ]
+        return acc, tail
+
+    acc, tail = lax.fori_loop(
+        0, total // group, gather,
+        (jnp.zeros((local_y, atoms), f32), jnp.zeros((16, LANES), f32)),
+    )
     value = scale * jnp.sum(acc * rows_y, axis=0, keepdims=True)
     out_ref[...] = jnp.broadcast_to(value, out_ref.shape)
-    tail = jnp.zeros((16, LANES), f32)
-    for q in range(owners):
-        tail = tail + got_ref[q, rows : rows + 16, :].astype(f32)
     energy_ref[...] = jnp.broadcast_to(escale * jnp.sum(tail, axis=0, keepdims=True), energy_ref.shape)
+
+    def leave(k, carry):
+        to, move = first(k)
+        guarded(to < owners, lambda: move.wait_send())
+        move_two = second(k)[1]
+        guarded(me < owners, lambda: move_two.wait_send())
+        return carry
+
+    lax.fori_loop(1, total, leave, 0)
 
 
 def influence_of(index_x, index_y, index_z, size_x, size_y, size_z, points):
@@ -501,18 +508,6 @@
     here = lax.axis_index("gx") * local[0] + jnp.arange(local[0], dtype=jnp.int32)
     wave_x = cas(order, here, size[0])
     charges = charge[:, 0, :].reshape(1, atoms)
-    payload = pl.pallas_call(
-        functools.partial(spread_kernel, (local[0], local[1], local[2], pack)),
-        out_shape=jax.ShapeDtypeStruct((owners * rows, LANES), bf16),
-        scratch_shapes=[
-            pltpu.VMEM((size[0], atoms), f32),
-            pltpu.VMEM((owners * rows, atoms), bf16),
-        ],
-        compiler_params=params(),
-        name="spread",
-    )(corner, fraction, charges, wave_x).reshape(owners, rows, LANES)
-    got = exchange_planes(payload, 2, counts, devices, owners)
-
     range_y = jnp.arange(size[1], dtype=jnp.int32)
     range_z = jnp.arange(size[2], dtype=jnp.int32)
     cas_z = cas(range_z, range_z, size[2]).reshape(counts[2], 1, local[2], size[2])
@@ -535,27 +530,30 @@
         index_x[:, None, None], range_y[None, :, None], range_z[None, None, :], *size, PC
     ).reshape(planes * size[1], size[2])
     each = counts[1] * counts[2]
-    solved = pl.pallas_call(
-        functools.partial(plane_kernel, (counts[1], counts[2], pack), counts[0]),
-        out_shape=jax.ShapeDtypeStruct((each, rows + 16, LANES), bf16),
-        compiler_params=params(),
-        name="planes",
-    )(got, wide_z, wide_y, influence)
-    field = exchange_planes(solved, 3, counts, owners, devices)
-
     potential, energy = pl.pallas_call(
         functools.partial(
-            field_kernel,
-            (local[0], local[1], local[2], pack, rows),
+            mesh_kernel,
+            counts,
+            local,
+            pack,
+            owners,
             coupling / volume,
             coupling / (2.0 * volume * atoms * devices),
-            owners,
         ),
         out_shape=(jax.ShapeDtypeStruct((8, atoms), f32), jax.ShapeDtypeStruct((8, LANES), f32)),
-        scratch_shapes=[pltpu.VMEM((size[0], atoms), f32)],
-        compiler_params=params(),
-        name="field",
-    )(corner, fraction, wave_x, field)
+        scratch_shapes=[
+            pltpu.VMEM((size[0], atoms), f32),
+            pltpu.VMEM((owners * rows, atoms), bf16),
+            pltpu.VMEM((pack, LANES, atoms), bf16),
+            pltpu.VMEM((owners, rows, LANES), bf16),
+            pltpu.VMEM((devices, rows, LANES), bf16),
+            pltpu.VMEM((each, rows + 16, LANES), bf16),
+            pltpu.VMEM((devices, rows + 16, LANES), bf16),
+        ]
+        + [pltpu.SemaphoreType.DMA((devices,))] * 4,
+        compiler_params=params(collective_id=2, has_side_effects=True),
+        name="mesh",
+    )(corner, fraction, charges, wave_x, wide_z, wide_y, influence)
     potential = potential[0].reshape(cells + (slots,))
 
     pre = preact.reshape(features.shape)

time: 99.4 us -> 87.7 us (0.88)
  Pallas kernels: 90.2 us -> 78.3 us
    pallas_call x5 -> x1, Pallas kernels: 38.8 us -> 28.7 us  [body(): pl.pallas_call(functools.partial(mesh_kernel, counts, local, pack, owners...]
    pallas_call x1, Pallas kernels: 10.1 us -> 8.21 us  [body(): pl.pallas_call(functools.partial(message_kernel, cells, counts), out_shap...]
where the time goes in v4:
time: 87.7 us; the launch traced here: 87.1 us
  Pallas kernels  78.3 us (89%)
  other arithmetic  3.55 us (4%)
  local copies, waits for them, and re-layouts  3.09 us (4%)
  matrix products  1.16 us (1%)
  between operations  1.05 us (1%)
    pallas_call x2, Pallas kernels, exchange_halo(): pl.pallas_call(functools.partial(halo_kernel, counts, lengths), out_shape...  33.4 us
    pallas_call x1, Pallas kernels, body(): pl.pallas_call(functools.partial(mesh_kernel, counts, local, pack, owners...  28.7 us
    pallas_call x1, Pallas kernels, body(): pl.pallas_call(functools.partial(message_kernel, cells, counts), out_shap...  8.21 us
    pallas_call x1, Pallas kernels, body(): pl.pallas_call(functools.partial(back_kernel, cells, counts), out_shape=j...  8.02 us

profile of v4, /device:TPU:0, one launch (start us, length us, event | category | flops | bytes accessed | tf_op | source)
XLA Modules:
  0.0 87.1 jit_solution(9157565592388131778)
XLA Ops:
  0.6 0.8 fusion.31
  1.4 0.2 concatenate.51.centre_ref
  1.7 1.2 %convolution_convert_fusion = bf16[1024,128]{1,0:T(8,128)(2,1)S(1)} fusion(bf16[1024,128]{1,0:T(8,128)(2,1)} %bitcast.54, bf16[128,128]{1,0:T(8,128)(2,1)} %msg_ref.1), kind=kOutput, calls=%fused_computation | convolution fusion | flops 33685504 | bytes 557056 | tf_op jit(solution)/shard_map/dot_general | solution.py:459
  2.9 0.3 concatenate.57.src_ref
  3.2 19.0 %halo.2 = bf16[4,2,6,144,128]{4,3,2,1,0:T(8,128)(2,1)S(1)} custom-call(bf16[2,1,4,144,128]{4,3,2,1,0:T(8,128)(2,1)S(1)} %concatenate.57.src_ref), custom_call_target="tpu_custom_call" | custom-call | tf_op jit(solution)/shard_map/halo/pallas_call | solution.py:163
  22.3 0.2 slice.16.value_ref
  22.5 0.4 copy-done.7
  22.9 0.1 broadcast_in_dim.8.table_ref
  23.0 0.1 copy-done
  23.2 8.2 %message.1 = (f32[8,128,128]{2,1,0:T(8,128)S(1)}, f32[8,8,128]{2,1,0:T(8,128)S(1)}) custom-call(bf16[8,16,128]{2,1,0:T(8,128)(2,1)S(1)} %concatenate.51.centre_ref, bf16[27,16,128]{2,1,0:T(8,128)(2,1)S(1)} %broadcast_in_dim.8.table_ref, bf16[4,2,6,16,128]{4,3,2,1,0:T(8,128)(2,1)S(1)} %slice.15.near_ref, bf16[4,2,6,128,128]{4,3,2,1,0:T(8,128)(2,1)S(1)} %slice.16.value_ref, ...), custom_call_target="tpu_custom_call" | custom-call | tf_op jit(solution)/shard_map/message/pallas_call | solution.py:480
  31.8 0.1 fusion.6.g_ref
  32.1 0.1 add.236
  32.3 0.1 copy.53
  32.4 0.2 sine_add_fusion.1.wave_ref
  32.7 1.1 %sine_add_fusion = f32[4,1,64,256]{3,2,1,0:T(8,128)S(1)} fusion(s32[4,64]{1,0:T(4,128)S(1)} %multiply_add_fusion), kind=kLoop, calls=%fused_computation.13 | loop fusion | flops 983040 | bytes 263168 | tf_op jit(solution)/shard_map/add | solution.py:41
  33.9 0.2 sine_add_fusion.2
  34.1 0.1 multiply_bitcast_fusion
  34.3 0.2 reshape.564
  35.0 28.7 %mesh.1 = (f32[8,1024]{1,0:T(8,128)S(1)}, f32[8,128]{1,0:T(8,128)S(1)}) custom-call(s32[3,1024]{1,0:T(4,128)S(1)} %reshape.561.corner_ref, f32[3,1024]{1,0:T(4,128)S(1)} %reshape.562.fraction_ref, f32[1,1024]{1,0:T(1,128)S(1)} %slice_bitcast_fusion.charge_ref, f32[128,32]{1,0:T(8,128)S(1)} %sine_add_fusion.1.wave_ref, ...), custom_call_target="tpu_custom_call" | custom-call | tf_op jit(solution)/shard_map/mesh/pallas_call | solution.py:533
  63.7 0.2 multiply_convert_fusion.cot_ref
  63.9 0.2 multiply_convert_fusion.1.src_ref
  64.2 14.4 %halo.3.value_ref = bf16[4,2,6,128,128]{4,3,2,1,0:T(8,128)(2,1)S(1)} custom-call(bf16[2,1,4,128,128]{4,3,2,1,0:T(8,128)(2,1)S(1)} %multiply_convert_fusion.1.src_ref), custom_call_target="tpu_custom_call" | custom-call | tf_op jit(solution)/shard_map/halo/pallas_call | solution.py:163
  78.6 8.0 %back.1 = f32[8,128,128]{2,1,0:T(8,128)} custom-call(bf16[8,16,128]{2,1,0:T(8,128)(2,1)S(1)} %concatenate.51.centre_ref, bf16[27,16,128]{2,1,0:T(8,128)(2,1)S(1)} %broadcast_in_dim.8.table_ref, bf16[4,2,6,16,128]{4,3,2,1,0:T(8,128)(2,1)S(1)} %slice.15.near_ref, bf16[4,2,6,128,128]{4,3,2,1,0:T(8,128)(2,1)S(1)} %halo.3.value_ref, ...), custom_call_target="tpu_custom_call" | custom-call | tf_op jit(solution)/shard_map/back/pallas_call | solution.py:564
  86.6 0.5 slice.19
  (58 shorter events, 1.3 us)
Async XLA Ops:
  22.2 0.7 copy-start.7
  22.2 0.7 copy-start.6
  22.2 1.0 %copy-start = (bf16[2,1,4,128,128]{4,3,2,1,0:T(8,128)(2,1)S(1)}, bf16[2,1,4,128,128]{4,3,2,1,0:T(8,128)(2,1)}, u32[]{:S(2)}) copy-start(bf16[2,1,4,128,128]{4,3,2,1,0:T(8,128)(2,1)} %param.7) | copy-start | bytes 786436
  22.2 1.0 %copy-start.1 = (bf16[128,128]{1,0:T(8,128)(2,1)S(1)}, bf16[128,128]{1,0:T(8,128)(2,1)}, u32[]{:S(2)}) copy-start(bf16[128,128]{1,0:T(8,128)(2,1)} %self_ref.3) | copy-start | bytes 98308
  31.4 3.4 %copy-start.3 = (s32[2,1,4,3,128]{4,2,3,1,0:T(4,128)S(1)}, s32[2,1,4,3,128]{4,2,3,1,0:T(4,128)}, u32[]{:S(2)}) copy-start(s32[2,1,4,3,128]{4,2,3,1,0:T(4,128)} %param.11) | copy-start | bytes 36868
  31.4 3.5 %copy-start.4 = (f32[2,1,4,3,128]{4,2,3,1,0:T(4,128)S(1)}, f32[2,1,4,3,128]{4,2,3,1,0:T(4,128)}, u32[]{:S(2)}) copy-start(f32[2,1,4,3,128]{4,2,3,1,0:T(4,128)} %param.12) | copy-start | bytes 36868
  63.7 14.9 %copy-start.5 = (f32[1,1024]{1,0:T(1,128)}, f32[1,1024]{1,0:T(1,128)S(1)}, u32[]{:S(2)}) copy-start(f32[1,1024]{1,0:T(1,128)S(1)} %slice.18) | copy-start | bytes 12292
  63.7 14.9 %copy-start.2 = (bf16[128,128]{1,0:T(8,128)(2,1)S(1)}, bf16[128,128]{1,0:T(8,128)(2,1)}, u32[]{:S(2)}) copy-start(bf16[128,128]{1,0:T(8,128)(2,1)} %msg_ref.1) | copy-start | bytes 98308

commit v5 on v4

--- a/solution.py
+++ b/solution.py
@@ -19,14 +19,6 @@
 bf16 = jnp.bfloat16
 NT = (((1,), (1,)), ((), ()))
 TN = (((0,), (0,)), ((), ()))
-
-
-def full_spec(shape):
-    return pl.BlockSpec(shape, lambda *_: (0,) * len(shape))
-
-
-def cell_spec(shape):
-    return pl.BlockSpec((1,) + tuple(shape[1:]), lambda i: (i,) + (0,) * (len(shape) - 1))
 
 
 def split3(value):
@@ -98,7 +90,7 @@
     return padded, own, moves
 
 
-def halo_kernel(counts, lengths, src_ref, out_ref, send_sem, recv_sem, own_sem):
+def run_halo(counts, lengths, src_ref, out_ref, send_sem, recv_sem, own_sem, idle):
     padded, own, moves = halo_plan(counts, lengths)
     me = [lax.axis_index(a) for a in AXES]
 
@@ -137,6 +129,7 @@
     for which in ready:
         copies[which].start()
     keep.start()
+    idle()
     waited = set()
 
     def forward(which):
@@ -149,75 +142,138 @@
     for which, move in enumerate(moves):
         if which not in waited and any(m[4] == which for m in moves):
             forward(which)
-    for which in range(len(moves)):
-        if which not in waited:
-            copies[which].wait_recv()
-    for copy in copies:
-        copy.wait_send()
     keep.wait()
 
-
-def exchange_halo(shard, number, counts):
-    lengths = shard.shape[:3]
-    padded, _, moves = halo_plan(counts, lengths)
-    return pl.pallas_call(
-        functools.partial(halo_kernel, counts, lengths),
-        out_shape=jax.ShapeDtypeStruct(padded + shard.shape[3:], shard.dtype),
-        in_specs=[pl.BlockSpec(memory_space=pltpu.VMEM)],
-        out_specs=pl.BlockSpec(memory_space=pl.ANY),
-        scratch_shapes=[
-            pltpu.SemaphoreType.DMA((len(moves),)),
-            pltpu.SemaphoreType.DMA((len(moves),)),
-            pltpu.SemaphoreType.DMA,
-        ],
-        compiler_params=params(collective_id=number, has_side_effects=True),
-        name="halo",
-    )(shard)
-
-
-def pair_total(cells, counts, centre, table_ref, near_ref, value_ref):
-    index = pl.program_id(0)
-    at_z = index % cells[2]
-    at_y = index // cells[2] % cells[1]
-    at_x = index // (cells[2] * cells[1])
-    total = None
-
-    def cell_at(o):
-        return tuple(
-            base + slot(step, count, length)
-            for base, step, count, length in zip((at_x, at_y, at_z), o, counts, cells)
+    def arrive():
+        for which in range(len(moves)):
+            if which not in waited:
+                copies[which].wait_recv()
+
+    def leave():
+        for copy in copies:
+            copy.wait_send()
+
+    return arrive, leave
+
+
+def halo_scratch(shape, dtype, counts):
+    padded, _, moves = halo_plan(counts, shape[:3])
+    return [
+        pltpu.VMEM(padded + shape[3:], dtype),
+        pltpu.SemaphoreType.DMA((len(moves),)),
+        pltpu.SemaphoreType.DMA((len(moves),)),
+        pltpu.SemaphoreType.DMA,
+    ]
+
+
+def pair_part(cells, counts, centre_ref, table_ref, near_of, value_of, acc_ref, inner):
+    plane = cells[1] * cells[2]
+    for at_x in range(cells[0]):
+        chosen = [
+            (w, o) for w, o in enumerate(offsets()) if (0 <= at_x + o[0] < cells[0]) == inner
+        ]
+        if not chosen:
+            continue
+
+        def one(i, carry, at_x=at_x, chosen=chosen):
+            base = (at_x, lax.div(i, cells[2]), lax.rem(i, cells[2]))
+            cell = at_x * plane + i
+            centre = centre_ref[cell]
+            total = acc_ref[cell]
+            for which, o in chosen:
+                where = tuple(
+                    start + slot(step, count, length)
+                    for start, step, count, length in zip(base, o, counts, cells)
+                )
+                inside = lax.dot_general(
+                    centre, near_of(where) * table_ref[which], TN, preferred_element_type=f32
+                )
+                inside = jnp.maximum(inside, 0.0)
+                weight = (pair_scale * inside * inside).astype(bf16)
+                total = total + jnp.dot(weight, value_of(where), preferred_element_type=f32)
+            acc_ref[cell] = total
+            return carry
+
+        lax.fori_loop(0, plane, one, 0)
+
+
+def message_kernel(
+    cells, counts, slots, centre_ref, table_ref, src_ref, feature_ref, self_ref, read_ref,
+    pre_ref, charge_ref, near_ref,
+    pad_ref, send_sem, recv_sem, own_sem,
+):
+    number = cells[0] * cells[1] * cells[2]
+
+    def begin():
+        def one(i, carry):
+            pre_ref[i] = jnp.dot(feature_ref[i], self_ref[...], preferred_element_type=f32)
+            return carry
+
+        lax.fori_loop(0, number, one, 0)
+
+    arrive, leave = run_halo(counts, cells, src_ref, pad_ref, send_sem, recv_sem, own_sem, begin)
+
+    def near_of(where):
+        return pad_ref[where[0], where[1], where[2], slots:, :]
+
+    def value_of(where):
+        return pad_ref[where[0], where[1], where[2], :slots, :]
+
+    pair_part(cells, counts, centre_ref, table_ref, near_of, value_of, pre_ref, True)
+    arrive()
+    pair_part(cells, counts, centre_ref, table_ref, near_of, value_of, pre_ref, False)
+
+    def read(i, carry):
+        preact = pre_ref[i]
+        active = preact / (1.0 + jnp.exp(-preact))
+        charge_ref[i] = lax.dot_general(
+            read_ref[...], active, NT, precision=highest, preferred_element_type=f32
         )
-
-    for which, o in enumerate(offsets()):
-        near = near_ref[cell_at(o)] * table_ref[which]
-        inside = lax.dot_general(centre, near, TN, preferred_element_type=f32)
-        inside = jnp.maximum(inside, 0.0)
-        weight = (pair_scale * inside * inside).astype(bf16)
-        part = jnp.dot(weight, value_ref[cell_at(o)], preferred_element_type=f32)
-        total = part if total is None else total + part
-    return total
-
-
-def message_kernel(
-    cells, counts, centre_ref, table_ref, near_ref, value_ref, feature_ref, self_ref, read_ref, pre_ref, charge_ref
+        return carry
+
+    lax.fori_loop(0, number, read, 0)
+    near_ref[...] = pad_ref[:, :, :, slots:, :]
+    leave()
+
+
+def back_kernel(
+    cells, counts, centre_ref, table_ref, near_ref, src_ref, cot_ref, msg_ref, self_ref,
+    out_ref,
+    pad_ref, acc_ref, send_sem, recv_sem, own_sem,
 ):
-    message = pair_total(cells, counts, centre_ref[0], table_ref, near_ref, value_ref)
-    preact = jnp.dot(feature_ref[0], self_ref[...], preferred_element_type=f32) + message
-    pre_ref[0] = preact
-    active = preact / (1.0 + jnp.exp(-preact))
-    charge_ref[0] = lax.dot_general(
-        read_ref[...], active, NT, precision=highest, preferred_element_type=f32
-    )
-
-
-def back_kernel(
-    cells, counts, centre_ref, table_ref, near_ref, value_ref, cot_ref, msg_ref, self_ref, out_ref
-):
-    total = pair_total(cells, counts, centre_ref[0], table_ref, near_ref, value_ref)
-    grad = lax.dot_general(total.astype(bf16), msg_ref[...], NT, preferred_element_type=f32)
-    out_ref[0] = grad + lax.dot_general(
-        cot_ref[0], self_ref[...], NT, preferred_element_type=f32
-    )
+    number = cells[0] * cells[1] * cells[2]
+
+    def begin():
+        acc_ref[...] = jnp.zeros_like(acc_ref)
+
+        def one(i, carry):
+            out_ref[i] = lax.dot_general(
+                cot_ref[i], self_ref[...], NT, preferred_element_type=f32
+            )
+            return carry
+
+        lax.fori_loop(0, number, one, 0)
+
+    arrive, leave = run_halo(counts, cells, src_ref, pad_ref, send_sem, recv_sem, own_sem, begin)
+
+    def near_of(where):
+        return near_ref[where[0], where[1], where[2]]
+
+    def value_of(where):
+        return pad_ref[where[0], where[1], where[2]]
+
+    pair_part(cells, counts, centre_ref, table_ref, near_of, value_of, acc_ref, True)
+    arrive()
+    pair_part(cells, counts, centre_ref, table_ref, near_of, value_of, acc_ref, False)
+
+    def one(i, carry):
+        out_ref[i] = out_ref[i] + lax.dot_general(
+            acc_ref[i].astype(bf16), msg_ref[...], NT, preferred_element_type=f32
+        )
+        return carry
+
+    lax.fori_loop(0, number, one, 0)
+    leave()
 
 
 def spline(corner, fraction, points, start=0):
@@ -470,30 +526,23 @@
     ).astype(bf16).reshape(number, 16, slots)
     table = offset_table()
 
-    padded = exchange_halo(jnp.concatenate([projected, near], axis=3), 0, counts)
-    values = padded[:, :, :, :slots]
-    nears = padded[:, :, :, slots:]
+    source = jnp.concatenate([projected, near], axis=3)
+    padded = halo_plan(counts, cells)[0]
 
     read = jnp.broadcast_to(charge_weight.astype(f32)[None, :], (8, width))
     cell_features = features.reshape(number, slots, width)
     square = (number, slots, width)
-    preact, charge = pl.pallas_call(
-        functools.partial(message_kernel, cells, counts),
-        out_shape=(jax.ShapeDtypeStruct(square, f32), jax.ShapeDtypeStruct((number, 8, slots), f32)),
-        grid=(number,),
-        in_specs=[
-            cell_spec(centre.shape),
-            full_spec(table.shape),
-            full_spec(nears.shape),
-            full_spec(values.shape),
-            cell_spec(square),
-            full_spec(self_weight.shape),
-            full_spec(read.shape),
-        ],
-        out_specs=(cell_spec(square), cell_spec((number, 8, slots))),
-        compiler_params=params(),
+    preact, charge, nears = pl.pallas_call(
+        functools.partial(message_kernel, cells, counts, slots),
+        out_shape=(
+            jax.ShapeDtypeStruct(square, f32),
+            jax.ShapeDtypeStruct((number, 8, slots), f32),
+            jax.ShapeDtypeStruct(padded + near.shape[3:], bf16),
+        ),
+        scratch_shapes=halo_scratch(source.shape, bf16, counts),
+        compiler_params=params(collective_id=0, has_side_effects=True),
         name="message",
-    )(centre, table, nears, values, cell_features, self_weight, read)
+    )(centre, table, source, cell_features, self_weight, read)
 
     shift = jnp.stack(
         [lax.broadcasted_iota(jnp.int32, cells + (slots,), d) * PC for d in range(3)], axis=0
@@ -560,24 +609,14 @@
     sigma = jax.nn.sigmoid(pre)
     slope = sigma * (1.0 + pre * (1.0 - sigma))
     cotangent = (potential[..., None] * charge_weight.astype(f32) * slope).astype(bf16)
-    cots = exchange_halo(cotangent, 1, counts)
+    scratch = halo_scratch(cotangent.shape, bf16, counts)
     grad = pl.pallas_call(
         functools.partial(back_kernel, cells, counts),
         out_shape=jax.ShapeDtypeStruct(square, f32),
-        grid=(number,),
-        in_specs=[
-            cell_spec(centre.shape),
-            full_spec(table.shape),
-            full_spec(nears.shape),
-            full_spec(cots.shape),
-            cell_spec(square),
-            full_spec(msg_weight.shape),
-            full_spec(self_weight.shape),
-        ],
-        out_specs=cell_spec(square),
-        compiler_params=params(),
+        scratch_shapes=scratch[:1] + [pltpu.VMEM(square, f32)] + scratch[1:],
+        compiler_params=params(collective_id=1, has_side_effects=True),
         name="back",
-    )(centre, table, nears, cots, cotangent.reshape(square), msg_weight, self_weight)
+    )(centre, table, nears, cotangent, cotangent.reshape(square), msg_weight, self_weight)
     return (grad.reshape(features.shape), potential, energy[0, 0])
 
 

time: 87.7 us -> 89.4 us (1.019)
  local copies, waits for them, and re-layouts: 3.09 us -> 6.37 us
  Pallas kernels: 78.3 us -> 76.9 us
    pallas_call x3 -> x1, Pallas kernels: 41.6 us -> 27.1 us  [body(): pl.pallas_call(functools.partial(message_kernel, cells, counts, slots), o...]
    pallas_call x1, Pallas kernels: 8.02 us -> 22.4 us  [body(): pl.pallas_call(functools.partial(back_kernel, cells, counts), out_shape=j...]
    unnamed x16 -> x17, local copies, waits for them, and re-layouts: 0.65 us -> 4.13 us
    pallas_call x1, Pallas kernels: 28.7 us -> 27.4 us  [body(): pl.pallas_call(functools.partial(mesh_kernel, counts, local, pack, owners...]
where the time goes in v5:
time: 89.4 us; the launch traced here: 88.9 us
  Pallas kernels  76.9 us (86%)
  local copies, waits for them, and re-layouts  6.37 us (7%)
  other arithmetic  3.54 us (4%)
  matrix products  1.15 us (1%)
  between operations  0.96 us (1%)
    pallas_call x1, Pallas kernels, body(): pl.pallas_call(functools.partial(mesh_kernel, counts, local, pack, owners...  27.4 us
    pallas_call x1, Pallas kernels, body(): pl.pallas_call(functools.partial(message_kernel, cells, counts, slots), o...  27.1 us
    pallas_call x1, Pallas kernels, body(): pl.pallas_call(functools.partial(back_kernel, cells, counts), out_shape=j...  22.4 us
    unnamed x17, local copies, waits for them, and re-layouts  4.13 us

profile of v5, /device:TPU:0, one launch (start us, length us, event | category | flops | bytes accessed | tf_op | source)
XLA Modules:
  0.0 88.9 jit_solution(6295123699934936276)
XLA Ops:
  0.6 0.8 fusion.31
  1.4 0.2 concatenate.51.centre_ref
  1.6 0.6 copy-done.1
  2.2 1.2 %convolution_convert_fusion = bf16[1024,128]{1,0:T(8,128)(2,1)S(1)} fusion(bf16[1024,128]{1,0:T(8,128)(2,1)} %bitcast.55, bf16[128,128]{1,0:T(8,128)(2,1)S(1)} %copy-done.1), kind=kOutput, calls=%fused_computation | convolution fusion | flops 33685504 | bytes 557056 | tf_op jit(solution)/shard_map/dot_general | solution.py:515
  3.5 0.3 concatenate.57.src_ref
  3.8 0.6 copy-done.7
  4.4 0.1 broadcast_in_dim.8.table_ref
  4.6 0.6 copy-done.2
  5.2 27.1 %message.1 = (f32[8,128,128]{2,1,0:T(8,128)S(1)}, f32[8,8,128]{2,1,0:T(8,128)S(1)}, bf16[4,2,6,16,128]{4,3,2,1,0:T(8,128)(2,1)S(1)}) custom-call(bf16[8,16,128]{2,1,0:T(8,128)(2,1)S(1)} %concatenate.51.centre_ref, bf16[27,16,128]{2,1,0:T(8,128)(2,1)S(1)} %broadcast_in_dim.8.table_ref, bf16[2,1,4,144,128]{4,3,2,1,0:T(8,128)(2,1)S(1)} %concatenate.57.src_ref, ...), custom_call_target="tpu_custom_call" | custom-call | tf_op jit(solution)/shard_map/message/pallas_call | solution.py:535
  32.6 0.5 copy-done.3
  33.1 0.7 copy-done.4
  34.0 0.1 add.236
  34.3 0.2 sine_add_fusion.1.wave_ref
  34.6 1.1 %sine_add_fusion = f32[4,1,64,256]{3,2,1,0:T(8,128)S(1)} fusion(s32[4,64]{1,0:T(4,128)S(1)} %multiply_add_fusion), kind=kLoop, calls=%fused_computation.13 | loop fusion | flops 983040 | bytes 263168 | tf_op jit(solution)/shard_map/add | solution.py:33
  35.9 0.2 sine_add_fusion.2
  36.1 0.1 multiply_bitcast_fusion
  36.2 0.2 reshape.564
  37.0 27.4 %mesh.1 = (f32[8,1024]{1,0:T(8,128)S(1)}, f32[8,128]{1,0:T(8,128)S(1)}) custom-call(s32[3,1024]{1,0:T(4,128)S(1)} %reshape.562.corner_ref, f32[3,1024]{1,0:T(4,128)S(1)} %reshape.563.fraction_ref, f32[1,1024]{1,0:T(1,128)S(1)} %slice_bitcast_fusion.charge_ref, f32[128,32]{1,0:T(8,128)S(1)} %sine_add_fusion.1.wave_ref, ...), custom_call_target="tpu_custom_call" | custom-call | tf_op jit(solution)/shard_map/mesh/pallas_call | solution.py:582
  64.4 0.2 multiply_convert_fusion.1.src_ref
  64.6 0.3 copy-done.5
  65.0 0.2 multiply_convert_fusion.cot_ref
  65.2 22.4 %back.1 = f32[8,128,128]{2,1,0:T(8,128)S(1)} custom-call(bf16[8,16,128]{2,1,0:T(8,128)(2,1)S(1)} %concatenate.51.centre_ref, bf16[27,16,128]{2,1,0:T(8,128)(2,1)S(1)} %broadcast_in_dim.8.table_ref, bf16[4,2,6,16,128]{4,3,2,1,0:T(8,128)(2,1)S(1)} %get-tuple-element.8.near_ref, bf16[2,1,4,128,128]{4,3,2,1,0:T(8,128)(2,1)S(1)} %multiply_convert_fusion.1.src_ref, ...), custom_call_target="tpu_custom_call" | custom-call | tf_op jit(solution)/shard_map/back/pallas_call | solution.py:613
  87.6 0.5 slice.11
  88.1 0.8 copy.80
  (55 shorter events, 1.4 us)
Async XLA Ops:
  1.4 0.8 copy-start.1
  3.4 1.0 %copy-start.6 = (bf16[27,16]{1,0:T(8,128)(2,1)S(1)}, bf16[27,16]{1,0:T(8,128)(2,1)}, u32[]{:S(2)}) copy-start(bf16[27,16]{1,0:T(8,128)(2,1)} %constant.125) | copy-start | bytes 2596
  3.4 1.1 %copy-start = (bf16[2,1,4,128,128]{4,3,2,1,0:T(8,128)(2,1)S(1)}, bf16[2,1,4,128,128]{4,3,2,1,0:T(8,128)(2,1)}, u32[]{:S(2)}) copy-start(bf16[2,1,4,128,128]{4,3,2,1,0:T(8,128)(2,1)} %param.7) | copy-start | bytes 786436
  3.8 0.7 copy-start.7
  4.4 0.8 copy-start.2
  32.3 0.7 copy-start.3
  33.1 0.7 copy-start.4
  64.4 0.6 copy-start.5

commit v6 on v5

--- a/solution.py
+++ b/solution.py
@@ -3,6 +3,7 @@
 
 import jax
 import jax.numpy as jnp
+import numpy as np
 from jax import lax
 from jax.experimental import pallas as pl
 from jax.experimental.pallas import tpu as pltpu
@@ -29,8 +30,8 @@
 
 
 def cas(first, second, length):
-    angle = 2.0 * math.pi / length * (first[:, None] * second[None, :] % length).astype(f32)
-    return jnp.cos(angle) + jnp.sin(angle)
+    angle = 2.0 * np.pi / length * (first[:, None] * second[None, :] % length)
+    return (np.cos(angle) + np.sin(angle)).astype(np.float32)
 
 
 def offsets():
@@ -43,7 +44,8 @@
         norm = float(o[0] ** 2 + o[1] ** 2 + o[2] ** 2)
         doubled = [2.0 * v for v in o]
         rows.append([1.0] * 6 + doubled + [1.0] * 3 + [-v for v in doubled] + [-norm])
-    return jnp.broadcast_to(jnp.array(rows, f32)[:, :, None], (27, 16, LANES)).astype(bf16)
+    table = np.broadcast_to(np.array(rows, np.float32)[:, :, None], (27, 16, LANES))
+    return jnp.asarray(table).astype(bf16)
 
 
 def slot(offset, devices, length):
@@ -194,7 +196,7 @@
             acc_ref[cell] = total
             return carry
 
-        lax.fori_loop(0, plane, one, 0)
+        lax.fori_loop(0, plane, one, 0, unroll=4)
 
 
 def message_kernel(
@@ -209,7 +211,7 @@
             pre_ref[i] = jnp.dot(feature_ref[i], self_ref[...], preferred_element_type=f32)
             return carry
 
-        lax.fori_loop(0, number, one, 0)
+        lax.fori_loop(0, number, one, 0, unroll=4)
 
     arrive, leave = run_halo(counts, cells, src_ref, pad_ref, send_sem, recv_sem, own_sem, begin)
 
@@ -231,7 +233,7 @@
         )
         return carry
 
-    lax.fori_loop(0, number, read, 0)
+    lax.fori_loop(0, number, read, 0, unroll=4)
     near_ref[...] = pad_ref[:, :, :, slots:, :]
     leave()
 
@@ -252,7 +254,7 @@
             )
             return carry
 
-        lax.fori_loop(0, number, one, 0)
+        lax.fori_loop(0, number, one, 0, unroll=4)
 
     arrive, leave = run_halo(counts, cells, src_ref, pad_ref, send_sem, recv_sem, own_sem, begin)
 
@@ -272,7 +274,7 @@
         )
         return carry
 
-    lax.fori_loop(0, number, one, 0)
+    lax.fori_loop(0, number, one, 0, unroll=4)
     leave()
 
 
@@ -550,28 +552,26 @@
     corner = (spline_corner.transpose(3, 0, 1, 2, 4) + shift).reshape(3, atoms)
     fraction = spline_fraction.transpose(3, 0, 1, 2, 4).reshape(3, atoms)
     order = (
-        jnp.arange(pack, dtype=jnp.int32)[:, None, None] * inner
-        + jnp.arange(owners, dtype=jnp.int32)[None, :, None] * planes
-        + jnp.arange(inner, dtype=jnp.int32)[None, None, :]
+        np.arange(pack)[:, None, None] * inner
+        + np.arange(owners)[None, :, None] * planes
+        + np.arange(inner)[None, None, :]
     ).reshape(-1)
-    here = lax.axis_index("gx") * local[0] + jnp.arange(local[0], dtype=jnp.int32)
-    wave_x = cas(order, here, size[0])
+    waves = cas(np.arange(size[0]), order, size[0]).reshape(counts[0], local[0], size[0])
+    wave_x = lax.dynamic_index_in_dim(
+        jnp.asarray(waves.transpose(0, 2, 1)), lax.axis_index("gx"), 0, keepdims=False
+    )
     charges = charge[:, 0, :].reshape(1, atoms)
     range_y = jnp.arange(size[1], dtype=jnp.int32)
     range_z = jnp.arange(size[2], dtype=jnp.int32)
-    cas_z = cas(range_z, range_z, size[2]).reshape(counts[2], 1, local[2], size[2])
-    blank = jnp.zeros_like(cas_z)
-    wide_z = jnp.concatenate(
-        [
-            jnp.concatenate([cas_z if at == h else blank for at in range(pack)], axis=2)
-            for h in range(pack)
-        ],
-        axis=1,
-    )
-    cas_y = cas(range_y, range_y, size[1]).reshape(size[1], counts[1], local[1])
-    same = jnp.eye(planes, dtype=f32).reshape(pack, inner, pack, inner)
-    wide_y = jnp.einsum("abcd,kgy->abkcgdy", same, cas_y, precision=highest).reshape(
-        planes * size[1], planes * size[1]
+    cas_z = cas(np.arange(size[2]), np.arange(size[2]), size[2])
+    wide_z = np.zeros((counts[2], pack, pack, local[2], size[2]), np.float32)
+    for h in range(pack):
+        wide_z[:, h, h] = cas_z.reshape(counts[2], local[2], size[2])
+    wide_z = jnp.asarray(wide_z.reshape(counts[2], pack, pack * local[2], size[2]))
+    cas_y = cas(np.arange(size[1]), np.arange(size[1]), size[1]).reshape(size[1], counts[1], local[1])
+    same = np.eye(planes, dtype=np.float32).reshape(pack, inner, pack, inner)
+    wide_y = jnp.asarray(
+        np.einsum("abcd,kgy->abkcgdy", same, cas_y).reshape(planes * size[1], planes * size[1])
     )
     me = lax.axis_index(AXES)
     index_x = me * planes + jnp.arange(planes, dtype=jnp.int32)

time: 89.4 us -> 78.6 us (0.88)
  Pallas kernels: 76.9 us -> 67.5 us
  other arithmetic: 3.54 us -> 1.48 us
    pallas_call x1, Pallas kernels: 22.4 us -> 17.4 us  [body(): pl.pallas_call(functools.partial(back_kernel, cells, counts), out_shape=j...]
    pallas_call x1, Pallas kernels: 27.1 us -> 22.1 us  [body(): pl.pallas_call(functools.partial(message_kernel, cells, counts, slots), o...]
    add x6 -> x0, other arithmetic: 1.66 us -> none  [the longest x3 1.51 us: cas(): return jnp.cos(angle) + jnp.sin(angle)]
    unnamed x17 -> x21, local copies, waits for them, and re-layouts: 4.13 us -> 4.52 us
where the time goes in v6:
time: 78.6 us; the launch traced here: 78.1 us
  Pallas kernels  67.5 us (86%)
  local copies, waits for them, and re-layouts  7.05 us (9%)
  other arithmetic  1.48 us (2%)
  matrix products  1.24 us (2%)
  between operations  0.87 us (1%)
    pallas_call x1, Pallas kernels, body(): pl.pallas_call(functools.partial(mesh_kernel, counts, local, pack, owners...  28 us
    pallas_call x1, Pallas kernels, body(): pl.pallas_call(functools.partial(message_kernel, cells, counts, slots), o...  22.1 us
    pallas_call x1, Pallas kernels, body(): pl.pallas_call(functools.partial(back_kernel, cells, counts), out_shape=j...  17.4 us
    unnamed x21, local copies, waits for them, and re-layouts  4.52 us

profile of v6, /device:TPU:0, one launch (start us, length us, event | category | flops | bytes accessed | tf_op | source)
XLA Modules:
  0.0 78.1 jit_solution(8851642466858488517)
XLA Ops:
  0.6 0.8 fusion.17
  1.5 0.2 concatenate.42.centre_ref
  1.7 0.5 copy-done.2
  2.2 1.2 %convolution_convert_fusion = bf16[1024,128]{1,0:T(8,128)(2,1)S(1)} fusion(bf16[1024,128]{1,0:T(8,128)(2,1)} %bitcast.53, bf16[128,128]{1,0:T(8,128)(2,1)S(1)} %copy-done.2), kind=kOutput, calls=%fused_computation | convolution fusion | flops 33685504 | bytes 557056 | tf_op jit(solution)/shard_map/dot_general | solution.py:517
  3.5 0.3 concatenate.48.src_ref
  3.9 0.3 copy-done.9
  4.2 0.1 broadcast.259.table_ref
  4.3 0.2 copy-done
  4.5 0.5 copy-done.3
  4.9 22.1 %message.1 = (f32[8,128,128]{2,1,0:T(8,128)S(1)}, f32[8,8,128]{2,1,0:T(8,128)S(1)}, bf16[4,2,6,16,128]{4,3,2,1,0:T(8,128)(2,1)S(1)}) custom-call(bf16[8,16,128]{2,1,0:T(8,128)(2,1)S(1)} %concatenate.42.centre_ref, bf16[27,16,128]{2,1,0:T(8,128)(2,1)S(1)} %broadcast.259.table_ref, bf16[2,1,4,144,128]{4,3,2,1,0:T(8,128)(2,1)S(1)} %concatenate.48.src_ref, ...), custom_call_target="tpu_custom_call" | custom-call | tf_op jit(solution)/shard_map/message/pallas_call | solution.py:537
  27.3 0.5 copy-done.5
  27.9 0.7 copy-done.6
  28.6 0.9 %dynamic-slice_bitcast_fusion.wave_ref = f32[128,32]{1,0:T(8,128)S(1)} fusion(f32[4,128,32]{2,1,0:T(8,128)} %constant.73.clone, s32[]{:T(128)S(6)} %select_n.40), kind=kLoop, calls=%fused_computation.9 | loop fusion | bytes 32772 | tf_op jit(solution)/shard_map/jit(dynamic_index_in_dim)/squeeze | solution.py:560
  29.5 0.1 add.124
  29.6 0.1 add.126
  29.7 0.1 fusion.g_ref
  29.9 0.7 copy-done.4
  30.6 28.0 %mesh.1 = (f32[8,1024]{1,0:T(8,128)S(1)}, f32[8,128]{1,0:T(8,128)S(1)}) custom-call(s32[3,1024]{1,0:T(4,128)S(1)} %reshape.397.corner_ref, f32[3,1024]{1,0:T(4,128)S(1)} %reshape.398.fraction_ref, f32[1,1024]{1,0:T(1,128)S(1)} %slice_bitcast_fusion.charge_ref, f32[128,32]{1,0:T(8,128)S(1)} %dynamic-slice_bitcast_fusion.wave_ref, ...), custom_call_target="tpu_custom_call" | custom-call | tf_op jit(solution)/shard_map/mesh/pallas_call | solution.py:582
  58.6 0.2 multiply_convert_fusion.1.src_ref
  58.9 0.3 copy-done.7
  59.2 0.2 multiply_convert_fusion.cot_ref
  59.4 17.4 %back.1 = f32[8,128,128]{2,1,0:T(8,128)S(1)} custom-call(bf16[8,16,128]{2,1,0:T(8,128)(2,1)S(1)} %concatenate.42.centre_ref, bf16[27,16,128]{2,1,0:T(8,128)(2,1)S(1)} %broadcast.259.table_ref, bf16[4,2,6,16,128]{4,3,2,1,0:T(8,128)(2,1)S(1)} %get-tuple-element.8.near_ref, bf16[2,1,4,128,128]{4,3,2,1,0:T(8,128)(2,1)S(1)} %multiply_convert_fusion.1.src_ref, ...), custom_call_target="tpu_custom_call" | custom-call | tf_op jit(solution)/shard_map/back/pallas_call | solution.py:613
  76.8 0.5 slice.11
  77.3 0.8 %copy.78 = f32[2,1,4,128,128]{4,3,2,1,0:T(8,128)} copy(f32[2,1,4,128,128]{4,3,2,1,0:T(8,128)S(1)} %bitcast.52) | data formatting | bytes 1048576
  (41 shorter events, 0.6 us)
Async XLA Ops:
  1.4 0.8 copy-start.2
  1.4 2.7 %copy-start.8 = (bf16[27,16]{1,0:T(8,128)(2,1)S(1)}, bf16[27,16]{1,0:T(8,128)(2,1)}, u32[]{:S(2)}) copy-start(bf16[27,16]{1,0:T(8,128)(2,1)} %constant.79) | copy-start | bytes 2596
  2.2 27.7 %copy-start.1 = (f32[4,2,128,256]{3,2,1,0:T(8,128)S(1)}, f32[4,2,128,256]{3,2,1,0:T(8,128)}, u32[]{:S(2)}) copy-start(f32[4,2,128,256]{3,2,1,0:T(8,128)} %constant.74.clone.z_ref) | copy-start | bytes 3145732
  3.5 0.7 copy-start.9
  3.5 1.0 %copy-start = (bf16[2,1,4,128,128]{4,3,2,1,0:T(8,128)(2,1)S(1)}, bf16[2,1,4,128,128]{4,3,2,1,0:T(8,128)(2,1)}, u32[]{:S(2)}) copy-start(bf16[2,1,4,128,128]{4,3,2,1,0:T(8,128)(2,1)} %param.10) | copy-start | bytes 786436
  4.2 0.8 copy-start.3
  27.0 0.7 copy-start.5
  27.8 0.7 copy-start.6
  29.7 0.8 %copy-start.4 = (f32[128,128]{1,0:T(8,128)S(1)}, f32[128,128]{1,0:T(8,128)}, u32[]{:S(2)}) copy-start(f32[128,128]{1,0:T(8,128)} %constant.75.clone.y_ref) | copy-start | bytes 196612
  58.6 0.6 copy-start.7
